TPU v7x, 32 devices: a whole 2x2x4 slice. The times are simulated.
32 devices in a mesh: dp: 16 (over z, y, core), tensor: 2 (over x).
Axes of the slice: x: 2, y: 2, z: 4, core: 2. Of those that a mesh axis runs over, the one named last changes fastest.
Arguments:
- tokens: bfloat16 [4096, 768], P(('dp', 'tensor')), may hold values from -6 to 6
- segments: int32 [4096], P('dp'), may hold values from 0 to 4095, as said below
- positions: int32 [4096], P('dp'), may hold values from 0 to 255, as said below
- cotangent: bfloat16 [4096, 768], P(('dp', 'tensor')), may hold values from -6 to 6
- qkv_weight: bfloat16 [1, 768, 2304], P(None, 'dp', 'tensor'), may hold values from -1 to 1
- qkv_bias: bfloat16 [1, 2304], P(None, ('tensor', 'dp')), may hold values from -3 to 3
- out_weight: bfloat16 [1, 768, 768], P(None, 'tensor', 'dp'), may hold values from -0.625 to 0.625
- out_bias: bfloat16 [1, 768], P(None, 'dp'), may hold values from -3 to 3
- up_weight: bfloat16 [1, 768, 3072], P(None, 'dp', 'tensor'), may hold values from -0.21875 to 0.21875
- up_bias: bfloat16 [1, 3072], P(None, ('tensor', 'dp')), may hold values from -3 to 3
- down_weight: bfloat16 [1, 3072, 768], P(None, 'tensor', 'dp'), may hold values from -0.109375 to 0.109375
- down_bias: bfloat16 [1, 768], P(None, 'dp'), may hold values from -3 to 3
- norm1_gain: bfloat16 [1, 768], P(None, 'dp'), may hold values from 0.5 to 1.5
- norm1_bias: bfloat16 [1, 768], P(None, 'dp'), may hold values from -2 to 2
- norm2_gain: bfloat16 [1, 768], P(None, 'dp'), may hold values from 0.5 to 1.5
- norm2_bias: bfloat16 [1, 768], P(None, 'dp'), may hold values from -2 to 2
Outputs:
- hidden_out: bfloat16 [1, 4096, 768], P(None, ('dp', 'tensor'))
- input_grad: float32 [4096, 768], P(('dp', 'tensor'))
- grad_qkv_weight: float32 [1, 768, 2304], P(None, 'dp', 'tensor')
- grad_qkv_bias: float32 [1, 2304], P(None, ('tensor', 'dp'))
- grad_out_weight: float32 [1, 768, 768], P(None, 'tensor', 'dp')
- grad_out_bias: float32 [1, 768], P(None, 'dp')
- grad_up_weight: float32 [1, 768, 3072], P(None, 'dp', 'tensor')
- grad_up_bias: float32 [1, 3072], P(None, ('tensor', 'dp'))
- grad_down_weight: float32 [1, 3072, 768], P(None, 'tensor', 'dp')
- grad_down_bias: float32 [1, 768], P(None, 'dp')
- grad_norm1_gain: float32 [1, 768], P(None, 'dp')
- grad_norm1_bias: float32 [1, 768], P(None, 'dp')
- grad_norm2_gain: float32 [1, 768], P(None, 'dp')
- grad_norm2_bias: float32 [1, 768], P(None, 'dp')
Inputs may be any that keep to these rules, and one draw needn't show every extreme that they name: `segments`: segment numbers never fall along the array, a new segment begins at the first token of every sequence of 256 tokens, and the last token of the array forms a segment of its own. `positions`: A token's position is its distance to the first token of its segment.
All inputs are finite; a program needn't handle non-finite values.
Results may differ from a plain program's by a relative error of at most 0.0094.
Values may be sent and summed in bfloat16 or wider, within the bound.
A program may use at most 128 MiB of HBM per device.

v0:
```python
import jax
import jax.numpy as jnp
from jax import lax
from jax.sharding import PartitionSpec as P

HEAD = 64
ROT = 16


EPS = 1e-05


def rotary_tables(pos_ids):
    half_rot = ROT // 2
    freq_index = jnp.arange(half_rot, dtype=jnp.float32)
    inverse = jnp.power(jnp.float32(10000.0), -2.0 * freq_index / ROT)
    angles = pos_ids.astype(jnp.float32)[:, None] * inverse[None, :]
    cos_tab = jnp.concatenate([jnp.cos(angles), jnp.cos(angles)], axis=1)
    sin_tab = jnp.concatenate([jnp.sin(angles), jnp.sin(angles)], axis=1)
    return (cos_tab, sin_tab)


def rotate(values, cos_tab, sin_tab):
    half_rot = ROT // 2
    rotary = values[..., :ROT]
    turned = jnp.concatenate([-rotary[..., half_rot:], rotary[..., :half_rot]], axis=-1)
    rotated = rotary * cos_tab[:, None, :] + turned * sin_tab[:, None, :]
    return jnp.concatenate([rotated, values[..., ROT:]], axis=-1)


def unrotate(grad_vals, cos_tab, sin_tab):
    half_rot = ROT // 2
    rotary = grad_vals[..., :ROT]
    scaled = rotary * sin_tab[:, None, :]
    back_part = jnp.concatenate([scaled[..., half_rot:], -scaled[..., :half_rot]], axis=-1)
    return jnp.concatenate(
        [rotary * cos_tab[:, None, :] + back_part, grad_vals[..., ROT:]], axis=-1
    )


def layernorm(values, gain_row, bias_row):
    centre = values - jnp.mean(values, axis=-1, keepdims=True)
    inv_std = lax.rsqrt(jnp.mean(centre * centre, axis=-1, keepdims=True) + EPS)
    normed = centre * inv_std
    return (normed * gain_row + bias_row, normed, inv_std)


def norm_back(upstream, normed, inv_std, gain_row):
    scaled = upstream * gain_row
    mean_term = jnp.mean(scaled, axis=-1, keepdims=True)
    proj_term = jnp.mean(scaled * normed, axis=-1, keepdims=True)
    grad_in = inv_std * (scaled - mean_term - normed * proj_term)
    return (grad_in, jnp.sum(upstream * normed, axis=0), jnp.sum(upstream, axis=0))


def gelu_slope(hidden_pre):
    cumul_part = 0.5 * (1.0 + jax.scipy.special.erf(hidden_pre * 0.7071067811865476))
    return cumul_part + hidden_pre * jnp.exp(-0.5 * hidden_pre * hidden_pre) * 0.3989422804014327


def block_mask(row_start, block_rows, segment_ids):
    seq_len = segment_ids.shape[0]
    query_index = row_start + jnp.arange(block_rows, dtype=jnp.int32)
    key_index = jnp.arange(seq_len, dtype=jnp.int32)
    return (key_index[None, :] <= query_index[:, None]) & (
        segment_ids[:, None] == segment_ids[None, :]
    )


def block_scores(query_block, key_rot, allowed):
    scores = jnp.einsum(
        "qhd,khd->hqk", query_block, key_rot, preferred_element_type=jnp.float32
    ) * HEAD ** (-0.5)
    return jnp.where(allowed[None], scores, -jnp.inf)


def attend_blocks(query_rot, key_rot, value_rows, segment_ids):
    seq_len = query_rot.shape[0]
    block_rows = min(512, seq_len)
    block_count = seq_len // block_rows

    def one_block(block_idx):
        row_start = block_idx * block_rows
        scores = block_scores(query_rot, key_rot, block_mask(row_start, block_rows, segment_ids))
        row_peak = jnp.max(scores, axis=-1, keepdims=True)
        row_total = jnp.sum(jnp.exp(scores - row_peak), axis=-1, keepdims=True)
        log_total = row_peak + jnp.log(row_total)
        weights_bf = jnp.exp(scores - log_total).astype(jnp.bfloat16)
        attended = jnp.einsum(
            "hqk,khd->qhd", weights_bf, value_rows, preferred_element_type=jnp.float32
        ).astype(jnp.bfloat16)
        return (attended, log_total)

    attended, totals = lax.map(one_block, jnp.arange(block_count, dtype=jnp.int32))
    return (attended.reshape(seq_len, query_rot.shape[1], HEAD), totals)


def attend_back_blocks(
    query_rot, key_rot, value_rows, attended, attended_grad, totals, segment_ids
):
    seq_len = query_rot.shape[0]
    block_rows = min(512, seq_len)
    block_count = seq_len // block_rows
    zero_rows = jnp.zeros(key_rot.shape, jnp.float32)

    def one_block(carry_acc, inputs):
        key_acc, value_acc = carry_acc
        block_idx, total_block = inputs
        row_start = block_idx * block_rows
        allowed = block_mask(row_start, block_rows, segment_ids)
        scores = block_scores(query_rot, key_rot, allowed)
        weights_full = jnp.where(allowed[None], jnp.exp(scores - total_block), 0.0)
        weights_bf = weights_full.astype(jnp.bfloat16)
        row_delta = jnp.einsum(
            "qhd,qhd->hq", attended, attended_grad, preferred_element_type=jnp.float32
        )
        value_acc = value_acc + jnp.einsum(
            "hqk,qhd->khd", weights_bf, attended_grad, preferred_element_type=jnp.float32
        )
        weight_grad = jnp.einsum(
            "qhd,khd->hqk", attended_grad, value_rows, preferred_element_type=jnp.float32
        )
        score_grad = (weights_full * (weight_grad - row_delta[:, :, None]) * HEAD ** (-0.5)).astype(
            jnp.bfloat16
        )
        query_grad = jnp.einsum(
            "hqk,khd->qhd", score_grad, key_rot, preferred_element_type=jnp.float32
        )
        key_acc = key_acc + jnp.einsum(
            "hqk,qhd->khd", score_grad, query_rot, preferred_element_type=jnp.float32
        )
        return ((key_acc, value_acc), query_grad)

    (key_grad, value_grad), query_blocks = lax.scan(
        one_block, (zero_rows, zero_rows), (jnp.arange(block_count, dtype=jnp.int32), totals)
    )
    return (query_blocks.reshape(key_rot.shape), key_grad, value_grad)


def layer_forward(rows_in, gathered, segment_ids, cos_tab, sin_tab):
    qkv_w, qkv_b, out_w, up_w, up_b, down_w, small_rows = gathered
    small_vals = small_rows.astype(jnp.float32)
    residual = rows_in.astype(jnp.float32)
    normed_one, unit_one, inv_one = layernorm(residual, small_vals[0], small_vals[1])
    normed_two, unit_two, inv_two = layernorm(residual, small_vals[2], small_vals[3])
    full_one, full_two = (
        lax.all_gather(normed_one.astype(jnp.bfloat16), "tensor", axis=0, tiled=True),
        lax.all_gather(normed_two.astype(jnp.bfloat16), "tensor", axis=0, tiled=True),
    )
    seq_len = full_one.shape[0]
    head_count = qkv_w.shape[1] // (3 * HEAD)
    projected = jnp.dot(full_one, qkv_w, preferred_element_type=jnp.float32) + qkv_b.astype(
        jnp.float32
    )
    projected = projected.reshape(seq_len, head_count, 3, HEAD)
    query_rot = rotate(projected[:, :, 0], cos_tab, sin_tab).astype(jnp.bfloat16)
    key_rot = rotate(projected[:, :, 1], cos_tab, sin_tab).astype(jnp.bfloat16)
    value_rows = projected[:, :, 2].astype(jnp.bfloat16)
    attended, totals = attend_blocks(query_rot, key_rot, value_rows, segment_ids)
    attended_flat = attended.reshape(seq_len, head_count * HEAD)
    hidden_pre = jnp.dot(full_two, up_w, preferred_element_type=jnp.float32) + up_b.astype(
        jnp.float32
    )
    hidden_act = jax.nn.gelu(hidden_pre, approximate=False).astype(jnp.bfloat16)
    attn_part = jnp.dot(attended_flat, out_w, preferred_element_type=jnp.float32)
    mlp_part = jnp.dot(hidden_act, down_w, preferred_element_type=jnp.float32)
    attn_rows, mlp_rows = (
        lax.psum_scatter(attn_part, "tensor", scatter_dimension=0, tiled=True),
        lax.psum_scatter(mlp_part, "tensor", scatter_dimension=0, tiled=True),
    )
    mixed_rows = attn_rows + mlp_rows
    output = (residual + mixed_rows + small_vals[4] + small_vals[5]).astype(jnp.bfloat16)
    saved_state = (
        unit_one,
        inv_one,
        unit_two,
        inv_two,
        full_one,
        full_two,
        query_rot,
        key_rot,
        value_rows,
        attended,
        totals,
        hidden_pre,
        hidden_act,
    )
    return (output, saved_state)


def flat_blocks(values, group_count):
    return values.reshape(group_count, -1)


def summed_blocks(received, rows_shape):
    return jnp.sum(received, axis=0).reshape(rows_shape)


def layer_backward(upstream, saved_state, gathered, segment_ids, cos_tab, sin_tab):
    qkv_w, qkv_b, out_w, up_w, up_b, down_w, small_rows = gathered
    small_vals = small_rows.astype(jnp.float32)
    (
        unit_one,
        inv_one,
        unit_two,
        inv_two,
        full_one,
        full_two,
        query_rot,
        key_rot,
        value_rows,
        attended,
        totals,
        hidden_pre,
        hidden_act,
    ) = saved_state
    seq_len = full_one.shape[0]
    head_count = query_rot.shape[1]
    group_count = lax.axis_size("dp")
    bias_grad = jnp.sum(upstream, axis=0)
    upstream_full = lax.all_gather(upstream.astype(jnp.bfloat16), "tensor", axis=0, tiled=True)
    grad_down_t = jnp.dot(upstream_full.T, hidden_act, preferred_element_type=jnp.float32)
    hidden_grad = (
        jnp.dot(upstream_full, down_w.T, preferred_element_type=jnp.float32)
        * gelu_slope(hidden_pre)
    ).astype(jnp.bfloat16)
    grad_up = jnp.dot(full_two.T, hidden_grad, preferred_element_type=jnp.float32)
    grad_upbias = jnp.sum(hidden_grad.astype(jnp.float32), axis=0)
    two_part = jnp.dot(hidden_grad, up_w.T, preferred_element_type=jnp.float32)
    attended_flat = attended.reshape(seq_len, head_count * HEAD)
    grad_out_t = jnp.dot(upstream_full.T, attended_flat, preferred_element_type=jnp.float32)
    attended_grad = (
        jnp.dot(upstream_full, out_w.T, preferred_element_type=jnp.float32)
        .astype(jnp.bfloat16)
        .reshape(seq_len, head_count, HEAD)
    )
    query_grad, key_grad, value_grad = attend_back_blocks(
        query_rot, key_rot, value_rows, attended, attended_grad, totals, segment_ids
    )
    stacked = jnp.stack(
        [unrotate(query_grad, cos_tab, sin_tab), unrotate(key_grad, cos_tab, sin_tab), value_grad],
        axis=2,
    )
    stacked = stacked.reshape(seq_len, head_count * 3 * HEAD).astype(jnp.bfloat16)
    grad_qkv = jnp.dot(full_one.T, stacked, preferred_element_type=jnp.float32)
    grad_qkvbias = jnp.sum(stacked.astype(jnp.float32), axis=0)
    one_part = jnp.dot(stacked, qkv_w.T, preferred_element_type=jnp.float32)
    one_grad, two_grad = (
        lax.psum_scatter(one_part, "tensor", scatter_dimension=0, tiled=True),
        lax.psum_scatter(two_part, "tensor", scatter_dimension=0, tiled=True),
    )
    in_one, gain_one_grad, bias_one_grad = norm_back(one_grad, unit_one, inv_one, small_vals[0])
    in_two, gain_two_grad, bias_two_grad = norm_back(two_grad, unit_two, inv_two, small_vals[2])
    rows_grad = upstream + in_one + in_two
    small_grads = jnp.stack(
        [gain_one_grad, bias_one_grad, gain_two_grad, bias_two_grad, bias_grad], axis=1
    )
    members = (grad_qkv, grad_qkvbias, grad_out_t, grad_up, grad_upbias, grad_down_t, small_grads)
    received = lax.all_to_all(
        tuple((flat_blocks(member, group_count) for member in members)),
        "dp",
        split_axis=0,
        concat_axis=0,
        tiled=True,
    )
    reduced = []
    for member, arrived in zip(members, received):
        reduced.append(summed_blocks(arrived, (member.shape[0] // group_count,) + member.shape[1:]))
    small_done = lax.psum(reduced[6], "tensor")
    return (
        rows_grad,
        (reduced[0], reduced[1], reduced[2].T, reduced[3], reduced[4], reduced[5].T, small_done.T),
    )


def on_device(
    tokens,
    segments,
    positions,
    cotangent,
    qkv_weight,
    qkv_bias,
    out_weight,
    out_bias,
    up_weight,
    up_bias,
    down_weight,
    down_bias,
    norm1_gain,
    norm1_bias,
    norm2_gain,
    norm2_bias,
):
    layer_count = qkv_weight.shape[0]
    cos_tab, sin_tab = rotary_tables(positions)
    small_local = [
        jnp.stack(
            [norm1_gain[0], norm1_bias[0], norm2_gain[0], norm2_bias[0], out_bias[0], down_bias[0]]
        )
    ]
    current = tokens
    layer_idx = 0
    gathered = (
        lax.all_gather(qkv_weight[layer_idx], "dp", axis=0, tiled=True),
        lax.all_gather(qkv_bias[layer_idx], "dp", axis=0, tiled=True),
        lax.all_gather(out_weight[layer_idx], "dp", axis=1, tiled=True),
        lax.all_gather(up_weight[layer_idx], "dp", axis=0, tiled=True),
        lax.all_gather(up_bias[layer_idx], "dp", axis=0, tiled=True),
        lax.all_gather(down_weight[layer_idx], "dp", axis=1, tiled=True),
        lax.all_gather(small_local[layer_idx], "dp", axis=1, tiled=True),
    )
    kept_weights = [gathered]
    current, saved_state = layer_forward(current, gathered, segments, cos_tab, sin_tab)
    outputs = [current]
    saves = [saved_state]
    upstream = cotangent.astype(jnp.float32)
    layer_grads = [None] * layer_count
    for layer_idx in reversed(range(layer_count)):
        gathered = kept_weights[layer_idx]
        upstream, layer_grads[layer_idx] = layer_backward(
            upstream, saves[layer_idx], gathered, segments, cos_tab, sin_tab
        )

    def stacked_grad(member):
        return jnp.stack([layer_grads[0][member]])

    small_all = stacked_grad(6)
    return (
        jnp.stack(outputs),
        upstream,
        stacked_grad(0),
        stacked_grad(1),
        stacked_grad(2),
        small_all[:, 4],
        stacked_grad(3),
        stacked_grad(4),
        stacked_grad(5),
        small_all[:, 4],
        small_all[:, 0],
        small_all[:, 1],
        small_all[:, 2],
        small_all[:, 3],
    )


def solution(mesh):
    in_specs = (
        P(("dp", "tensor"), None),
        P("dp"),
        P("dp"),
        P(("dp", "tensor"), None),
        P(None, "dp", "tensor"),
        P(None, ("tensor", "dp")),
        P(None, "tensor", "dp"),
        P(None, "dp"),
        P(None, "dp", "tensor"),
        P(None, ("tensor", "dp")),
        P(None, "tensor", "dp"),
        P(None, "dp"),
        P(None, "dp"),
        P(None, "dp"),
        P(None, "dp"),
        P(None, "dp"),
    )
    out_specs = (
        P(None, ("dp", "tensor"), None),
        P(("dp", "tensor"), None),
        P(None, "dp", "tensor"),
        P(None, ("tensor", "dp")),
        P(None, "tensor", "dp"),
        P(None, "dp"),
        P(None, "dp", "tensor"),
        P(None, ("tensor", "dp")),
        P(None, "tensor", "dp"),
        P(None, "dp"),
        P(None, "dp"),
        P(None, "dp"),
        P(None, "dp"),
        P(None, "dp"),
    )
    return jax.shard_map(
        on_device, mesh=mesh, in_specs=in_specs, out_specs=out_specs, check_vma=False
    )
```

profile of v0, /device:TPU:13, one launch (start us, length us, event | category | flops | bytes accessed | tf_op | source)
XLA Modules:
  0.0 529.9 jit_solution(11499641870161937213)
XLA Ops:
  9.5 6.7 %all_gather.39 = bf16[256,768]{1,0:T(8,128)(2,1)S(1)} all-gather(bf16[128,768]{1,0:T(8,128)(2,1)} %param.19), channel_id=1, replica_groups=mesh['dp'=16,'tensor'=2] {'tensor'}, dimensions={0}, use_global_device_ids=true | all-gather | bytes 589824 | tf_op jit(solution)/shard_map/all_gather | solution.py:221
  16.2 19.2 %all-gather.2 = bf16[1,384,768]{1,2,0:T(8,128)(2,1)S(1)} all-gather(bf16[1,384,48]{1,2,0:T(8,128)(2,1)} %param.22), channel_id=4, replica_groups=mesh['dp'=16,'tensor'=2] {'dp'}, dimensions={2}, use_global_device_ids=true | all-gather | bytes 626688 | tf_op jit(solution)/shard_map/all_gather | solution.py:306
  36.1 20.9 %all-gather.6 = bf16[16,48,6]{1,2,0:T(8,128)(2,1)S(1)} all-gather(bf16[1,48,6]{1,2,0:T(8,128)(2,1)S(1)} %bitcast.127), channel_id=1, replica_groups=mesh['dp'=16,'tensor'=2] {'dp'}, dimensions={0}, use_global_device_ids=true | all-gather | bytes 9792 | tf_op jit(solution)/shard_map/all_gather | solution.py:310
  58.6 7.0 %all_gather.31 = bf16[256,768]{1,0:T(8,128)(2,1)S(1)} all-gather(bf16[128,768]{1,0:T(8,128)(2,1)S(1)} %get-tuple-element.101), channel_id=1, replica_groups=mesh['dp'=16,'tensor'=2] {'tensor'}, dimensions={0}, use_global_device_ids=true | all-gather | bytes 589824 | tf_op jit(solution)/shard_map/all_gather | solution.py:147
  68.1 24.4 %all-reduce.2 = (bf16[1536]{0:T(1024)(128)(2,1)S(1)}, bf16[1152]{0:T(1024)(128)(2,1)S(1)}) all-reduce(bf16[1536]{0:T(1024)(128)(2,1)S(1)} %dynamic-update-slice.1, bf16[1152]{0:T(1024)(128)(2,1)S(1)} %dynamic-update-slice), channel_id=6, replica_groups=mesh['dp'=16,'tensor'=2] {'dp'}, use_global_device_ids=true, to_apply=%add.1 | all-reduce | flops 2688 | bytes 10752
  92.7 6.4 %all_gather.35 = bf16[256,768]{1,0:T(8,128)(2,1)S(1)} all-gather(bf16[128,768]{1,0:T(8,128)(2,1)S(1)} %get-tuple-element.102), channel_id=1, replica_groups=mesh['dp'=16,'tensor'=2] {'tensor'}, dimensions={0}, use_global_device_ids=true | all-gather | bytes 589824 | tf_op jit(solution)/shard_map/all_gather | solution.py:148
  99.2 3.2 convolution_add_fusion
  111.3 6.7 %fusion.12 = (bf16[256,1536]{1,0:T(8,128)(2,1)}, f32[256,1536]{1,0:T(8,128)}) fusion(f32[1536]{0:T(1024)S(1)} %convert_element_type.103, bf16[256,768]{1,0:T(8,128)(2,1)S(1)} %all_gather.35, bf16[1,768,1536]{2,1,0:T(8,128)(2,1)} %all-gather.13.cloned.1.call-done), kind=kOutput, calls=%fused_computation.18 | convolution fusion | flops 629932032 | bytes 5117952 | tf_op jit(solution)/shard_map/dot_general | solution.py:161
  118.0 20.3 %all-gather.15.cloned.1.call-done = bf16[1,1536,768]{1,2,0:T(8,128)(2,1)} async-done(((bf16[1,1536,48]{1,2,0:T(8,128)(2,1)}), bf16[1,1536,768]{1,2,0:T(8,128)(2,1)}) %all-gather.15.cloned.1.call-update) | async-done | bytes 2359312 | tf_op jit(solution)/shard_map/all_gather | solution.py:309
  138.2 3.3 convert_reduce_fusion
  144.9 5.4 %all-to-all-start.1 = ((f32[16,1,72]{2,1,0:T(1,128)}), f32[16,1,72]{2,1,0:T(1,128)S(1)}, u32[]{:S(2)}, u32[]{:S(2)}) async-start(f32[16,1,72]{2,1,0:T(1,128)} %bitcast.31), calls=%async_computation.3 | async-start | bytes 16384 | tf_op jit(solution)/shard_map/all_to_all | solution.py:259
  150.9 3.2 all-to-all-done.1
  154.1 5.9 %all-to-all-start.5 = ((f32[16,1,96]{2,1,0:T(1,128)}), f32[16,1,96]{2,1,0:T(1,128)S(1)}, u32[]{:S(2)}, u32[]{:S(2)}) async-start(f32[16,1,96]{2,1,0:T(1,128)} %all_to_all.52), calls=%async_computation.7 | async-start | bytes 16384 | tf_op jit(solution)/shard_map/all_to_all | solution.py:259
  163.9 6.2 %all-to-all-start.2 = ((f32[16,1,18432]{2,1,0:T(1,128)}), f32[16,1,18432]{2,1,0:T(1,128)S(1)}, u32[]{:S(2)}, u32[]{:S(2)}) async-start(f32[16,1,18432]{2,1,0:T(1,128)} %all_to_all.57), calls=%async_computation.4 | async-start | bytes 2359296 | tf_op jit(solution)/shard_map/all_to_all | solution.py:259
  178.9 18.1 %reduce-scatter.8.cloned.1.call-done = f32[128,768]{1,0:T(8,128)} async-done(((f32[256,768]{1,0:T(8,128)}), f32[128,768]{1,0:T(8,128)}) %reduce-scatter.8.cloned.1.call-update) | async-done | bytes 393232 | tf_op jit(solution)/shard_map/reduce_scatter | solution.py:168
  201.4 6.5 %all-to-all-start.3 = ((f32[16,1,240]{2,1,0:T(1,128)}), f32[16,1,240]{2,1,0:T(1,128)S(1)}, u32[]{:S(2)}, u32[]{:S(2)}) async-start(f32[16,1,240]{2,1,0:T(1,128)} %all_to_all.58), calls=%async_computation.5 | async-start | bytes 32768 | tf_op jit(solution)/shard_map/all_to_all | solution.py:259
  209.8 5.3 all_to_all.56
  215.1 6.0 %all-to-all-start = ((f32[16,1,55296]{2,1,0:T(1,128)}), f32[16,1,55296]{2,1,0:T(1,128)S(1)}, u32[]{:S(2)}, u32[]{:S(2)}) async-start(f32[16,1,55296]{2,1,0:T(1,128)} %all_to_all.56), calls=%async_computation.2 | async-start | bytes 7077888 | tf_op jit(solution)/shard_map/all_to_all | solution.py:259
  221.1 4.2 fusion.78
  225.3 12.8 %all_to_all.59 = f32[16,1,73728]{2,1,0:T(1,128)} reshape(f32[768,1536]{1,0:T(8,128)} %fusion.78) | data formatting | bytes 9437184 | tf_op jit(solution)/shard_map/all_to_all | solution.py:259
  238.1 61.4 %all-to-all-done = f32[16,1,55296]{2,1,0:T(1,128)S(1)} async-done(((f32[16,1,55296]{2,1,0:T(1,128)}), f32[16,1,55296]{2,1,0:T(1,128)S(1)}, u32[]{:S(2)}, u32[]{:S(2)}) %all-to-all-start) | async-done | bytes 3538976 | tf_op jit(solution)/shard_map/all_to_all | solution.py:259
  299.4 4.8 all-to-all-start.4
  304.2 4.3 convolution_bitcast_fusion
  308.5 6.1 %copy.178 = f32[768,1536]{1,0:T(8,128)} copy(f32[768,1536]{0,1:T(8,128)} %convolution_bitcast_fusion) | data formatting | bytes 9437184 | tf_op jit(solution)/shard_map/dot_general | solution.py:222
  314.6 12.7 %all_to_all.60 = f32[16,1,73728]{2,1,0:T(1,128)} reshape(f32[768,1536]{1,0:T(8,128)} %copy.178) | data formatting | bytes 9437184 | tf_op jit(solution)/shard_map/all_to_all | solution.py:259
  327.3 80.6 %all-to-all-done.4 = f32[16,1,73728]{2,1,0:T(1,128)} async-done(((f32[16,1,73728]{2,1,0:T(1,128)}), f32[16,1,73728]{2,1,0:T(1,128)}, u32[]{:S(2)}, u32[]{:S(2)}) %all-to-all-start.4) | async-done | bytes 4718624 | tf_op jit(solution)/shard_map/all_to_all | solution.py:259
  407.9 4.8 all-to-all-start.6
  421.3 7.3 %psum.7 = f32[1,5,48]{1,2,0:T(8,128)} all-reduce(f32[1,5,48]{1,2,0:T(8,128)} %bitcast.123), channel_id=1, replica_groups=mesh['dp'=16,'tensor'=2] {'tensor'}, use_global_device_ids=true, to_apply=%region_22.23 | all-reduce | flops 240 | bytes 1920 | tf_op jit(solution)/shard_map/psum | solution.py:269
  430.3 3.5 reduce_sum.205
  435.5 5.4 %reduce_sum.215 = f32[73728]{0:T(1024)S(1)} reduce(f32[16,1,73728]{2,1,0:T(1,128)} %all-to-all-done.4, f32[]{:T(128)} %constant.38.clone.1), dimensions={0,1}, to_apply=%region_23.24 | reduce | flops 1105920 | bytes 5013508 | tf_op jit(solution)/shard_map/reduce_sum | solution.py:196
  441.6 74.7 %all-to-all-done.6 = f32[16,1,73728]{2,1,0:T(1,128)} async-done(((f32[16,1,73728]{2,1,0:T(1,128)}), f32[16,1,73728]{2,1,0:T(1,128)}, u32[]{:S(2)}, u32[]{:S(2)}) %all-to-all-start.6) | async-done | bytes 4718624 | tf_op jit(solution)/shard_map/all_to_all | solution.py:259
  516.4 5.4 %reduce_sum.218 = f32[73728]{0:T(1024)S(1)} reduce(f32[16,1,73728]{2,1,0:T(1,128)} %all-to-all-done.6, f32[]{:T(128)} %constant.38.clone.1), dimensions={0,1}, to_apply=%region_26.27 | reduce | flops 1105920 | bytes 5013508 | tf_op jit(solution)/shard_map/reduce_sum | solution.py:196
  (170 shorter events, 51.3 us)
Async XLA Ops:
  7.2 28.8 %copy-start.23 = (bf16[1,48]{1,0:T(2,128)(2,1)S(1)}, bf16[1,48]{1,0:T(2,128)(2,1)}, u32[]{:S(2)}) copy-start(bf16[1,48]{1,0:T(2,128)(2,1)} %param.28) | copy-start | bytes 292
  7.2 28.8 %copy-start.24 = (bf16[1,48]{1,0:T(2,128)(2,1)S(1)}, bf16[1,48]{1,0:T(2,128)(2,1)}, u32[]{:S(2)}) copy-start(bf16[1,48]{1,0:T(2,128)(2,1)} %param.29) | copy-start | bytes 292
  7.2 28.8 %copy-start.25 = (bf16[1,48]{1,0:T(2,128)(2,1)S(1)}, bf16[1,48]{1,0:T(2,128)(2,1)}, u32[]{:S(2)}) copy-start(bf16[1,48]{1,0:T(2,128)(2,1)} %param.30) | copy-start | bytes 292
  7.2 28.8 %copy-start.26 = (bf16[1,48]{1,0:T(2,128)(2,1)S(1)}, bf16[1,48]{1,0:T(2,128)(2,1)}, u32[]{:S(2)}) copy-start(bf16[1,48]{1,0:T(2,128)(2,1)} %param.31) | copy-start | bytes 292
  7.2 28.8 %copy-start.27 = (bf16[1,48]{1,0:T(2,128)(2,1)S(1)}, bf16[1,48]{1,0:T(2,128)(2,1)}, u32[]{:S(2)}) copy-start(bf16[1,48]{1,0:T(2,128)(2,1)} %param.23) | copy-start | bytes 292
  7.2 28.8 %copy-start.28 = (bf16[1,48]{1,0:T(2,128)(2,1)S(1)}, bf16[1,48]{1,0:T(2,128)(2,1)}, u32[]{:S(2)}) copy-start(bf16[1,48]{1,0:T(2,128)(2,1)} %param.27) | copy-start | bytes 292
  7.2 91.9 %all-gather.11.cloned.1.call-start = ((), (), s32[]{:S(2)}) async-start(), calls=%async_computation.12 | async-start | bytes 1880064 | tf_op jit(solution)/shard_map/all_gather | solution.py:304
  8.0 103.3 %all-gather.13.cloned.1.call-start = ((), (), s32[]{:S(2)}) async-start(), calls=%async_computation.13 | async-start | bytes 2506752 | tf_op jit(solution)/shard_map/all_gather | solution.py:307
  8.7 49.0 %copy-start.2 = (bf16[128,768]{1,0:T(8,128)(2,1)S(1)}, bf16[128,768]{1,0:T(8,128)(2,1)}, u32[]{:S(2)}) copy-start(bf16[128,768]{1,0:T(8,128)(2,1)} %param.16) | copy-start | bytes 589828
  8.7 129.5 %all-gather.15.cloned.1.call-start = ((), (), s32[]{:S(2)}) async-start(), calls=%async_computation.14 | async-start | bytes 2506752 | tf_op jit(solution)/shard_map/all_gather | solution.py:309
  9.5 164.6 %reduce-scatter.4.cloned.1.call-start = ((), (), s32[]{:S(2)}) async-start(), calls=%async_computation.10 | async-start | bytes 1179648 | tf_op jit(solution)/shard_map/reduce_scatter | solution.py:249
  16.2 143.8 %copy-start = (bf16[256,768]{1,0:T(8,128)(2,1)}, bf16[256,768]{1,0:T(8,128)(2,1)S(1)}, u32[]{:S(2)}) copy-start(bf16[256,768]{1,0:T(8,128)(2,1)S(1)} %all_gather.39) | copy-start | bytes 1179652
  35.4 30.2 %copy-start.32 = (u32[32]{0:T(128)S(1)}, u32[32]{0:T(128)}, u32[]{:S(2)}) copy-start(u32[32]{0:T(128)} %constant.130) | copy-start | bytes 388
  35.4 32.1 %copy-start.30 = (bf16[1,96]{1,0:T(2,128)(2,1)S(1)}, bf16[1,96]{1,0:T(2,128)(2,1)}, u32[]{:S(2)}) copy-start(bf16[1,96]{1,0:T(2,128)(2,1)} %param.25) | copy-start | bytes 580
  35.4 32.4 %copy-start.31 = (bf16[1,72]{1,0:T(2,128)(2,1)S(1)}, bf16[1,72]{1,0:T(2,128)(2,1)}, u32[]{:S(2)}) copy-start(bf16[1,72]{1,0:T(2,128)(2,1)} %param.21) | copy-start | bytes 436
  35.5 57.0 %copy-start.21 = (s32[256]{0:T(256)S(1)}, s32[256]{0:T(256)}, u32[]{:S(2)}) copy-start(s32[256]{0:T(256)} %param.18) | copy-start | bytes 3076
  35.5 57.1 %copy-start.20 = (s32[256]{0:T(256)S(1)}, s32[256]{0:T(256)}, u32[]{:S(2)}) copy-start(s32[256]{0:T(256)} %param.17) | copy-start | bytes 3076
  65.6 33.6 %copy-start.9 = (bf16[256,768]{1,0:T(8,128)(2,1)}, bf16[256,768]{1,0:T(8,128)(2,1)S(1)}, u32[]{:S(2)}) copy-start(bf16[256,768]{1,0:T(8,128)(2,1)S(1)} %all_gather.31) | copy-start | bytes 1179652
  111.2 66.1 %reduce-scatter.6.cloned.1.call-start = ((), (), s32[]{:S(2)}) async-start(), calls=%async_computation.11 | async-start | bytes 1179648 | tf_op jit(solution)/shard_map/reduce_scatter | solution.py:250
  142.5 17.6 %copy-start.6 = (bf16[6,64,256]{2,1,0:T(8,128)(2,1)S(1)}, bf16[6,64,256]{2,1,0:T(8,128)(2,1)}, u32[]{:S(2)}) copy-start(bf16[6,64,256]{2,1,0:T(8,128)(2,1)} %get-tuple-element.121) | copy-start | bytes 589828
  144.9 9.2 %all-to-all-start.1 = ((f32[16,1,72]{2,1,0:T(1,128)}), f32[16,1,72]{2,1,0:T(1,128)S(1)}, u32[]{:S(2)}, u32[]{:S(2)}) async-start(f32[16,1,72]{2,1,0:T(1,128)} %bitcast.31), calls=%async_computation.3 | async-start | bytes 16384 | tf_op jit(solution)/shard_map/all_to_all | solution.py:259
  154.1 9.7 %all-to-all-start.5 = ((f32[16,1,96]{2,1,0:T(1,128)}), f32[16,1,96]{2,1,0:T(1,128)S(1)}, u32[]{:S(2)}, u32[]{:S(2)}) async-start(f32[16,1,96]{2,1,0:T(1,128)} %all_to_all.52), calls=%async_computation.7 | async-start | bytes 16384 | tf_op jit(solution)/shard_map/all_to_all | solution.py:259
  163.9 36.5 %all-to-all-start.2 = ((f32[16,1,18432]{2,1,0:T(1,128)}), f32[16,1,18432]{2,1,0:T(1,128)S(1)}, u32[]{:S(2)}, u32[]{:S(2)}) async-start(f32[16,1,18432]{2,1,0:T(1,128)} %all_to_all.57), calls=%async_computation.4 | async-start | bytes 2359296 | tf_op jit(solution)/shard_map/all_to_all | solution.py:259
  170.1 26.9 %reduce-scatter.8.cloned.1.call-start = ((), (), s32[]{:S(2)}) async-start(), calls=%async_computation.15 | async-start | bytes 1179648 | tf_op jit(solution)/shard_map/reduce_scatter | solution.py:168
  172.7 24.2 %copy-start.11 = (bf16[128,768]{1,0:T(8,128)(2,1)S(1)}, bf16[128,768]{1,0:T(8,128)(2,1)}, u32[]{:S(2)}) copy-start(bf16[128,768]{1,0:T(8,128)(2,1)} %param.19) | copy-start | bytes 589828
  172.7 24.2 %copy-start.14 = (f32[768]{0:T(1024)S(1)}, f32[768]{0:T(1024)}, u32[]{:S(2)}) copy-start(f32[768]{0:T(1024)} %get-tuple-element.85) | copy-start | bytes 9220
  172.7 24.2 %copy-start.15 = (f32[768]{0:T(1024)S(1)}, f32[768]{0:T(1024)}, u32[]{:S(2)}) copy-start(f32[768]{0:T(1024)} %get-tuple-element.86) | copy-start | bytes 9220
  201.4 13.7 %all-to-all-start.3 = ((f32[16,1,240]{2,1,0:T(1,128)}), f32[16,1,240]{2,1,0:T(1,128)S(1)}, u32[]{:S(2)}, u32[]{:S(2)}) async-start(f32[16,1,240]{2,1,0:T(1,128)} %all_to_all.58), calls=%async_computation.5 | async-start | bytes 32768 | tf_op jit(solution)/shard_map/all_to_all | solution.py:259
  215.1 84.3 %all-to-all-start = ((f32[16,1,55296]{2,1,0:T(1,128)}), f32[16,1,55296]{2,1,0:T(1,128)S(1)}, u32[]{:S(2)}, u32[]{:S(2)}) async-start(f32[16,1,55296]{2,1,0:T(1,128)} %all_to_all.56), calls=%async_computation.2 | async-start | bytes 7077888 | tf_op jit(solution)/shard_map/all_to_all | solution.py:259
  299.4 108.5 %all-to-all-start.4 = ((f32[16,1,73728]{2,1,0:T(1,128)}), f32[16,1,73728]{2,1,0:T(1,128)}, u32[]{:S(2)}, u32[]{:S(2)}) async-start(f32[16,1,73728]{2,1,0:T(1,128)} %all_to_all.59), calls=%async_computation.6 | async-start | bytes 9437184 | tf_op jit(solution)/shard_map/all_to_all | solution.py:259
  407.9 108.5 %all-to-all-start.6 = ((f32[16,1,73728]{2,1,0:T(1,128)}), f32[16,1,73728]{2,1,0:T(1,128)}, u32[]{:S(2)}, u32[]{:S(2)}) async-start(f32[16,1,73728]{2,1,0:T(1,128)} %all_to_all.60), calls=%async_computation.8 | async-start | bytes 9437184 | tf_op jit(solution)/shard_map/all_to_all | solution.py:259
  430.3 92.2 %copy-start.22 = (f32[48]{0:T(128)}, f32[48]{0:T(128)S(1)}, u32[]{:S(2)}) copy-start(f32[48]{0:T(128)S(1)} %get-tuple-element.84) | copy-start | bytes 580
  (14 other events, 55.7 us)
Sparse Core Ops, SparseCore 0:
  10.2 40.8 all-gather.10
  53.4 41.6 all-gather.12
  97.4 40.8 all-gather.14
  140.3 17.2 reduce-scatter.3
  159.7 17.5 reduce-scatter.5
  179.4 17.4 reduce-scatter.7
where the time goes:
time: 532 us; the launch traced here: 530 us
  waiting for transfers between devices  264 us (50%)
  blocking collectives  91.9 us (17%)
  local copies, waits for them, and re-layouts  57.9 us (11%)
  starting transfers between devices  39.8 us (7%)
  matrix products  34.5 us (6%)
  other arithmetic  25.2 us (5%)
  between operations  16.1 us (3%)
    all_to_all x7, waiting for transfers between devices, layer_backward(): lax.all_to_all(tuple((flat_blocks(member, group_count) for member in memb...  221 us
    all_to_all x7, starting transfers between devices, layer_backward(): lax.all_to_all(tuple((flat_blocks(member, group_count) for member in memb...  39.6 us
    all_to_all x7, local copies, waits for them, and re-layouts, layer_backward(): lax.all_to_all(tuple((flat_blocks(member, group_count) for member in memb...  35.2 us
    unnamed x1, blocking collectives  24.4 us
    all_gather x1, blocking collectives, on_device(): lax.all_gather(small_local[layer_idx], 'dp', axis=1, tiled=True)  20.9 us
    all_gather x1, waiting for transfers between devices, on_device(): lax.all_gather(down_weight[layer_idx], 'dp', axis=1, tiled=True)  20.3 us
    reduce_sum x7, other arithmetic, summed_blocks(): return jnp.sum(received, axis=0).reshape(rows_shape)  20 us
    all_gather x1, blocking collectives, on_device(): lax.all_gather(out_weight[layer_idx], 'dp', axis=1, tiled=True)  19.2 us
  transfers between devices with their start and end apart: 13, of which 8 were waited for; matrix products, arithmetic and copies ran while one was open for 14% of the time, Pallas kernels for 0%

commit v1 on v0

v1 whole, which is shorter than its diff:
```python
import functools

import jax
import jax.numpy as jnp
from jax import lax
from jax.experimental import pallas as pl
from jax.experimental.pallas import tpu as pltpu
from jax.sharding import PartitionSpec as P

HEAD = 64
ROT = 16
EPS = 1e-05
F32 = jnp.float32
BF16 = jnp.bfloat16
VMEM = pltpu.VMEM


def up128(n):
    return -(-n // 128) * 128


class Sizes:
    def __init__(self, rows, up_q, qkv_q, out_q, qkvb, upb):
        self.rows, self.up_q, self.qkv_q, self.out_q = rows, up_q, qkv_q, out_q
        self.qkvb, self.upb = qkvb, upb
        self.qb_cols, self.ub_cols = -(-qkvb // rows), -(-upb // rows)
        self.down = up_q
        self.qkv = 2 * up_q
        self.small = self.qkv + qkv_q
        self.n_small = 6 + self.qb_cols + self.ub_cols
        self.out = up128(self.small + self.n_small)
        self.cols = up128(self.out + out_q)
        self.tile = self.small // 128 * 128
        self.tile_end = self.out

    def pack(self, up, down, qkv, small, out):
        lead = up.shape[:-1]
        gap = self.out - self.small - small.shape[-1]
        tail = self.cols - self.out - self.out_q
        parts = [up, down, qkv, small, jnp.zeros(lead + (gap,), BF16), out]
        if tail:
            parts.append(jnp.zeros(lead + (tail,), BF16))
        return jnp.concatenate([p.astype(BF16) for p in parts], axis=-1)


def places(n_outer):
    dp = lax.axis_index("dp")
    x = lax.axis_index("tensor")
    core = lax.rem(dp, 2)
    chip = dp // 2
    inner = lax.rem(chip, 2)
    outer = chip // 2
    return dp, x, core, chip, inner, outer


def dev(chip, core, x):
    return {"dp": chip * 2 + core, "tensor": x}


def greet(partners, outer, n_outer, up, down):
    barrier = pltpu.get_barrier_semaphore()

    def tell(partner):
        pl.semaphore_signal(
            barrier, inc=1, device_id=partner, device_id_type=pl.DeviceIdType.MESH
        )

    for partner in partners:
        tell(partner)
    pl.when(outer < n_outer - 1)(lambda: tell(up))
    pl.when(outer > 0)(lambda: tell(down))
    chained = jnp.minimum(outer, 1) + jnp.minimum(n_outer - 1 - outer, 1)
    pl.semaphore_wait(barrier, len(partners) + chained)


def rcopy(src, dst, send, recv, where):
    return pltpu.make_async_remote_copy(
        src_ref=src,
        dst_ref=dst,
        send_sem=send,
        recv_sem=recv,
        device_id=where,
        device_id_type=pl.DeviceIdType.MESH,
    )


def partner_list(n_outer):
    dp, x, core, chip, inner, outer = places(n_outer)
    sibling = dev(chip, 1 - core, x)
    across = dev(chip, core, 1 - x)
    diagonal = dev(chip, 1 - core, 1 - x)
    inner_peer = dev(outer * 2 + 1 - inner, core, x)
    up = dev((outer + 1) * 2 + inner, core, x)
    down = dev((outer - 1) * 2 + inner, core, x)
    return sibling, across, diagonal, inner_peer, up, down


def gather_kernel(
    n_outer, p_ref, a_ref, w_ref, t_ref, loc_sem, grp_s, grp_r, sib_s, sib_r, ch_s, ch_r, in_s, in_r
):
    dp, x, core, chip, inner, outer = places(n_outer)
    sibling, across, diagonal, inner_peer, up, down = partner_list(n_outer)
    own_w = pltpu.make_async_copy(p_ref.at[core], w_ref.at[chip, core], loc_sem.at[0])
    own_t = pltpu.make_async_copy(a_ref, t_ref.at[core, x], loc_sem.at[1])
    own_w.start()
    own_t.start()
    greet([sibling, across, diagonal, inner_peer], outer, n_outer, up, down)
    sib = rcopy(p_ref.at[1 - core], w_ref.at[chip, core], sib_s, sib_r, sibling)
    sib.start()
    own_w.wait()
    sib.wait_recv()
    last = n_outer - 1

    def chain(way, step):
        block = outer - step if way == 0 else outer + step
        there = (outer < last) & (block >= 0) if way == 0 else (outer > 0) & (block <= last)
        spot = w_ref.at[block * 2 + inner]
        where = up if way == 0 else down
        return there, lambda: rcopy(spot, spot, ch_s.at[way, step], ch_r.at[way, step], where)

    def arrival(way, step):
        block = outer - 1 - step if way == 0 else outer + 1 + step
        there = block >= 0 if way == 0 else block <= last
        spot = w_ref.at[block * 2 + inner]
        return there, lambda: rcopy(spot, spot, ch_s.at[way, step], ch_r.at[way, step], up)

    def forward(way, step, mine):
        block = outer - 1 - step if way == 0 else outer + 1 + step
        there = block >= 0 if way == 0 else block <= last
        spot = w_ref.at[block * 2 + (inner if mine else 1 - inner)]
        return there, lambda: rcopy(spot, spot, in_s.at[way, step], in_r.at[way, step], inner_peer)

    def act(pair, what):
        there, copy = pair
        pl.when(there)(lambda: what(copy()))

    def start(copy):
        copy.start()

    for way in range(2):
        act(chain(way, 0), start)
    own = w_ref.at[chip]
    mine = rcopy(own, own, in_s.at[0, last], in_r.at[0, last], inner_peer)
    mine.start()
    group = []
    for slot, where in enumerate((sibling, across, diagonal)):
        copy = rcopy(a_ref, t_ref.at[core, x], grp_s.at[slot], grp_r.at[slot], where)
        copy.start()
        group.append(copy)
    for step in range(last):
        for way in range(2):
            act(arrival(way, step), lambda copy: copy.wait_recv())
            if step + 1 < last:
                act(chain(way, step + 1), start)
            act(forward(way, step, True), start)
    for copy in group:
        copy.wait_recv()
    mine.wait_recv()
    for step in range(last):
        for way in range(2):
            act(forward(way, step, False), lambda copy: copy.wait_recv())
    own_t.wait()
    sib.wait_send()
    mine.wait_send()
    for copy in group:
        copy.wait_send()
    for step in range(last):
        for way in range(2):
            act(chain(way, step), lambda copy: copy.wait_send())
            act(forward(way, step, True), lambda copy: copy.wait_send())


def scatter_kernel(
    sizes,
    n_outer,
    n2t_ref,
    cott_ref,
    n1t_ref,
    du_ref,
    act_ref,
    dqkv_ref,
    att_ref,
    small_ref,
    h_ref,
    r_ref,
    hs_ref,
    x_ref,
    first_buf,
    b1,
    send_buf,
    cbuf,
    acc,
    hr,
    small_out,
    small_in,
    grp_s,
    grp_r,
    in_s,
    in_r,
    ch_s,
    ch_r,
    sib_s,
    sib_r,
    sm_s,
    sm_r,
):
    dp, x, core, chip, inner, outer = places(n_outer)
    sibling, across, diagonal, inner_peer, up, down = partner_list(n_outer)
    last = n_outer - 1
    rows = sizes.rows
    lo, hi = sizes.tile, sizes.tile_end

    def block(target, put):
        def product(left, right):
            if rows % 16 == 0:
                lhs = left[target].reshape(2 * rows, -1)
                out = jnp.dot(lhs, right[...], preferred_element_type=F32)
                return out.reshape(2, rows, -1)
            return jnp.stack(
                [
                    jnp.dot(left[target, side], right[...], preferred_element_type=F32)
                    for side in range(2)
                ]
            )

        put(0, sizes.down, product(n2t_ref, du_ref))
        put(sizes.down, sizes.qkv, product(cott_ref, act_ref))
        part = product(n1t_ref, dqkv_ref)
        cut = lo - sizes.qkv
        put(sizes.qkv, lo, part[:, :, :cut])
        put(lo, hi, part[:, :, cut:] + small_ref[target])
        put(sizes.out, sizes.cols, product(cott_ref, att_ref))

    def to_acc(start, stop, value):
        acc[:, :, start:stop] = value

    greet([sibling, across, diagonal, inner_peer], outer, n_outer, up, down)
    group = []
    spots = ((sibling, 1 - core, x), (across, core, 1 - x), (diagonal, 1 - core, 1 - x))
    for slot, (where, to_core, to_x) in enumerate(spots):
        copy = rcopy(h_ref.at[to_core, to_x], hr.at[slot], grp_s.at[slot], grp_r.at[slot], where)
        copy.start()
        group.append(copy)

    def in_order(what):
        @pl.loop(0, last)
        def _(tick):
            back = last - tick
            pl.when(outer <= tick)(lambda: what(0, outer + back))
            pl.when(outer >= back)(lambda: what(1, outer - back))

    def exchange(target):
        return rcopy(
            first_buf.at[target], b1.at[target], in_s.at[target], in_r.at[target], inner_peer
        )

    def passing(way, target):
        return rcopy(
            send_buf.at[target],
            cbuf.at[way, target],
            ch_s.at[way, target],
            ch_r.at[way, target],
            up if way == 0 else down,
        )

    def send_first(target):
        def put(start, stop, value):
            first_buf[target, :, :, start:stop] = value.astype(BF16)

        block(target * 2 + 1 - inner, put)
        exchange(target).start()

    def send_second(way, target):
        block(target * 2 + inner, to_acc)
        exchange(target).wait_recv()
        acc[...] += b1[target].astype(F32)
        started = outer > 0 if way == 0 else outer < last

        @pl.when(started)
        def _():
            passing(way, target).wait_recv()
            acc[...] += cbuf[way, target].astype(F32)

        send_buf[target] = acc[...].astype(BF16)
        passing(way, target).start()

    in_order(lambda way, target: send_first(target))
    send_first(outer)
    in_order(send_second)
    for copy in group:
        copy.wait_recv()
    hs_ref[...] = (
        h_ref[core, x].astype(F32)
        + hr[0].astype(F32)
        + hr[1].astype(F32)
        + hr[2].astype(F32)
    )
    block(chip, to_acc)
    exchange(outer).wait_recv()
    acc[...] += b1[outer].astype(F32)
    for way in range(2):

        @pl.when(outer > 0 if way == 0 else outer < last)
        def _():
            passing(way, outer).wait_recv()
            acc[...] += cbuf[way, outer].astype(F32)

    sib = rcopy(acc.at[1 - core], r_ref.at[core], sib_s, sib_r, sibling)
    sib.start()
    r_ref[core] = acc[core]
    sib.wait_recv()
    small_out[...] = r_ref[0, :, lo:hi] + r_ref[1, :, lo:hi]
    small = rcopy(small_out, small_in, sm_s, sm_r, across)
    small.start()
    small.wait_recv()
    x_ref[0] = small_out[...]
    x_ref[1] = small_out[...] + small_in[...]
    sib.wait_send()
    small.wait_send()
    for copy in group:
        copy.wait_send()
    exchange(outer).wait_send()

    def sent(way, target):
        exchange(target).wait_send()
        passing(way, target).wait_send()

    in_order(sent)


def gather(sizes, n_outer, packed, rows):
    dma = pltpu.SemaphoreType.DMA
    full = pl.BlockSpec(memory_space=VMEM)
    return pl.pallas_call(
        functools.partial(gather_kernel, n_outer),
        out_shape=(
            jax.ShapeDtypeStruct((2 * n_outer, 2) + packed.shape[1:], BF16),
            jax.ShapeDtypeStruct((2, 2) + rows.shape, BF16),
        ),
        in_specs=[full, full],
        out_specs=(full, full),
        scratch_shapes=[
            dma((2,)),
            dma((3,)),
            dma((3,)),
            dma,
            dma,
            dma((2, n_outer)),
            dma((2, n_outer)),
            dma((2, n_outer)),
            dma((2, n_outer)),
        ],
        compiler_params=pltpu.CompilerParams(
            collective_id=0, has_side_effects=True, vmem_limit_bytes=60 * 2**20
        ),
        name="gather",
    )(packed, rows)


def scatter(sizes, n_outer, operands, parts):
    dma = pltpu.SemaphoreType.DMA
    full = pl.BlockSpec(memory_space=VMEM)
    block = (2, sizes.rows, sizes.cols)
    width = sizes.tile_end - sizes.tile
    return pl.pallas_call(
        functools.partial(scatter_kernel, sizes, n_outer),
        out_shape=(
            jax.ShapeDtypeStruct(block, F32),
            jax.ShapeDtypeStruct(parts.shape[2:], F32),
            jax.ShapeDtypeStruct((2, sizes.rows, width), F32),
        ),
        in_specs=[full] * (len(operands) + 1),
        out_specs=(full, full, full),
        scratch_shapes=[
            VMEM((n_outer,) + block, BF16),
            VMEM((n_outer,) + block, BF16),
            VMEM((n_outer,) + block, BF16),
            VMEM((2, n_outer) + block, BF16),
            VMEM(block, F32),
            VMEM((3,) + parts.shape[2:], BF16),
            VMEM((sizes.rows, width), F32),
            VMEM((sizes.rows, width), F32),
            dma((3,)),
            dma((3,)),
            dma((n_outer,)),
            dma((n_outer,)),
            dma((2, n_outer)),
            dma((2, n_outer)),
            dma,
            dma,
            dma,
            dma,
        ],
        compiler_params=pltpu.CompilerParams(
            collective_id=1, has_side_effects=True, vmem_limit_bytes=60 * 2**20
        ),
        name="scatter",
    )(*operands, parts)


def rotary_tables(pos_ids):
    half_rot = ROT // 2
    freq_index = jnp.arange(half_rot, dtype=F32)
    inverse = jnp.power(F32(10000.0), -2.0 * freq_index / ROT)
    angles = pos_ids[..., None] * inverse
    cos_tab = jnp.concatenate([jnp.cos(angles), jnp.cos(angles)], axis=-1)
    sin_tab = jnp.concatenate([jnp.sin(angles), jnp.sin(angles)], axis=-1)
    return (cos_tab[:, None], sin_tab[:, None])


def rotate(values, cos_tab, sin_tab):
    half_rot = ROT // 2
    rotary = values[..., :ROT]
    turned = jnp.concatenate([-rotary[..., half_rot:], rotary[..., :half_rot]], axis=-1)
    return jnp.concatenate([rotary * cos_tab + turned * sin_tab, values[..., ROT:]], axis=-1)


def unrotate(grad_vals, cos_tab, sin_tab):
    half_rot = ROT // 2
    rotary = grad_vals[..., :ROT]
    scaled = rotary * sin_tab
    back_part = jnp.concatenate([scaled[..., half_rot:], -scaled[..., :half_rot]], axis=-1)
    return jnp.concatenate([rotary * cos_tab + back_part, grad_vals[..., ROT:]], axis=-1)


def unit_rows(values):
    centre = values - jnp.mean(values, axis=-1, keepdims=True)
    inv_std = lax.rsqrt(jnp.mean(centre * centre, axis=-1, keepdims=True) + EPS)
    return centre * inv_std, inv_std


def dot(a, b, ca, cb):
    return lax.dot_general(a, b, (((ca,), (cb,)), ((), ())), preferred_element_type=F32)


def fold(vector, count, rows, cols):
    per = vector.shape[0] // count
    padded = jnp.pad(vector.reshape(count, per), ((0, 0), (0, rows * cols - per)))
    return padded.reshape(count, rows, cols)


def on_device(
    tokens,
    segments,
    positions,
    cotangent,
    qkv_weight,
    qkv_bias,
    out_weight,
    out_bias,
    up_weight,
    up_bias,
    down_weight,
    down_bias,
    norm1_gain,
    norm1_bias,
    norm2_gain,
    norm2_bias,
):
    dp_size = lax.axis_size("dp")
    n_outer = dp_size // 4
    core = lax.rem(lax.axis_index("dp"), 2)
    x = lax.axis_index("tensor")
    own, width = tokens.shape
    rows = qkv_weight.shape[1]
    seq_len = segments.shape[0]
    qkv_q, up_q, out_q = (
        qkv_weight.shape[2] // 2,
        up_weight.shape[2] // 2,
        out_weight.shape[1] // 2,
    )
    sizes = Sizes(rows, up_q, qkv_q, out_q, qkv_bias.shape[1], up_bias.shape[1])
    heads = out_q // HEAD

    def halves(w):
        return jnp.swapaxes(w.reshape(rows, 2, -1), 0, 1)

    def halves_t(w):
        return jnp.swapaxes(w.reshape(2, -1, rows), 1, 2)

    small = jnp.concatenate(
        [
            jnp.stack(
                [
                    norm1_gain[0],
                    norm1_bias[0],
                    norm2_gain[0],
                    norm2_bias[0],
                    out_bias[0],
                    down_bias[0],
                ],
                axis=1,
            ),
            fold(qkv_bias[0], 1, rows, sizes.qb_cols)[0],
            fold(up_bias[0], 1, rows, sizes.ub_cols)[0],
        ],
        axis=1,
    )
    packed = sizes.pack(
        halves(up_weight[0]),
        halves_t(down_weight[0]),
        halves(qkv_weight[0]),
        jnp.broadcast_to(small[None], (2,) + small.shape),
        halves_t(out_weight[0]),
    )
    own_pos = lax.dynamic_slice_in_dim(positions, x * own, own, 0).astype(BF16)
    rows_in = jnp.concatenate(
        [tokens, cotangent, jnp.pad(own_pos[:, None], ((0, 0), (0, 127)))], axis=1
    )
    gathered, group_rows = gather(sizes, n_outer, packed, rows_in)

    flat = gathered.reshape(dp_size * rows, sizes.cols)
    up_w = flat[:, :up_q]
    down_wt = flat[:, up_q : 2 * up_q]
    qkv_w = flat[:, sizes.qkv : sizes.qkv + qkv_q]
    out_wt = flat[:, sizes.out : sizes.out + out_q]
    smalls = flat[:, sizes.small : sizes.small + sizes.n_small].astype(F32)
    vecs = smalls[:, :6].T
    by_dev = smalls.reshape(dp_size, rows, sizes.n_small)
    qb = by_dev[:, :, 6 : 6 + sizes.qb_cols].reshape(dp_size, -1)[:, : sizes.qkvb].reshape(-1)
    ub = by_dev[:, :, 6 + sizes.qb_cols :].reshape(dp_size, -1)[:, : sizes.upb].reshape(-1)
    qkv_b = lax.dynamic_slice_in_dim(qb, core * qkv_q, qkv_q, 0)
    up_b = lax.dynamic_slice_in_dim(ub, core * up_q, up_q, 0)

    group_rows = group_rows.reshape(4 * own, -1)
    count = 4 * own
    seqs = count // seq_len
    xs = group_rows[:, :width].astype(F32)
    cot = group_rows[:, width : 2 * width]
    pos = group_rows[:, 2 * width].astype(F32).reshape(seqs, seq_len)
    cos_tab, sin_tab = rotary_tables(pos)
    query_index = jnp.arange(seq_len, dtype=F32)
    key_index = query_index[None, None, :]
    first_key = query_index[None, :] - pos
    allowed = (
        (key_index <= query_index[None, :, None]) & (key_index >= first_key[:, :, None])
    )[:, None]

    unit, _ = unit_rows(xs)
    n1 = (unit * vecs[0] + vecs[1]).astype(BF16)
    n2 = (unit * vecs[2] + vecs[3]).astype(BF16)
    projected = (dot(n1, qkv_w, 1, 0) + qkv_b).reshape(seqs, seq_len, heads, 3, HEAD)
    projected = jnp.transpose(projected, (3, 0, 2, 1, 4))
    query = rotate(projected[0], cos_tab, sin_tab).astype(BF16)
    key = rotate(projected[1], cos_tab, sin_tab).astype(BF16)
    value = projected[2].astype(BF16)
    scale = HEAD ** (-0.5)

    def ein(spec, a, b):
        return jnp.einsum(spec, a, b, preferred_element_type=F32)

    scores = jnp.where(allowed, ein("shqd,shkd->shqk", query, key) * scale, -jnp.inf)
    peak = jnp.max(scores, axis=-1, keepdims=True)
    log_total = peak + jnp.log(jnp.sum(jnp.exp(scores - peak), axis=-1, keepdims=True))
    weights = jnp.exp(scores - log_total)
    weights_bf = weights.astype(BF16)
    attended = ein("shqk,shkd->shqd", weights_bf, value).astype(BF16)
    attended_flat = jnp.swapaxes(attended, 1, 2).reshape(count, out_q)
    pre = dot(n2, up_w, 1, 0) + up_b
    cumul = 0.5 * (1.0 + jax.scipy.special.erf(pre * 0.7071067811865476))
    act = (pre * cumul).astype(BF16)
    slope = cumul + pre * jnp.exp(-0.5 * pre * pre) * 0.3989422804014327
    mixed = dot(attended_flat, out_wt, 1, 1) + dot(act, down_wt, 1, 1)

    du = (dot(cot, down_wt, 1, 0) * slope).astype(BF16)
    g_upb = jnp.sum(du.astype(F32), axis=0)
    dn2 = dot(du, up_w, 1, 1)
    d_att = dot(cot, out_wt, 1, 0).astype(BF16).reshape(seqs, seq_len, heads, HEAD)
    d_att = jnp.swapaxes(d_att, 1, 2)
    delta = jnp.sum(attended.astype(F32) * d_att.astype(F32), axis=-1, keepdims=True)
    d_value = ein("shqk,shqd->shkd", weights_bf, d_att)
    d_weight = ein("shqd,shkd->shqk", d_att, value)
    d_score = (weights * (d_weight - delta) * scale).astype(BF16)
    d_query = unrotate(ein("shqk,shkd->shqd", d_score, key), cos_tab, sin_tab)
    d_key = unrotate(ein("shqk,shqd->shkd", d_score, query), cos_tab, sin_tab)
    d_qkv = jnp.stack([d_query, d_key, d_value], axis=0).astype(BF16)
    d_qkv = jnp.transpose(d_qkv, (1, 3, 2, 0, 4)).reshape(count, qkv_q)
    g_qkvb = jnp.sum(d_qkv.astype(F32), axis=0)
    dn1 = dot(d_qkv, qkv_w, 1, 1)
    back = dn1 * vecs[0] + dn2 * vecs[2]
    up_rows = cotangent.astype(F32)
    norm_rows = jnp.stack(
        [
            jnp.sum(dn1 * unit, axis=0),
            jnp.sum(dn1, axis=0),
            jnp.sum(dn2 * unit, axis=0),
            jnp.sum(dn2, axis=0),
            jnp.sum(up_rows, axis=0),
            jnp.zeros((width,), F32),
        ],
        axis=1,
    ).reshape(dp_size, rows, 6)
    own_half = jnp.arange(2)[:, None] == core
    qb_full = jnp.where(own_half, g_qkvb[None], 0.0).reshape(-1)
    ub_full = jnp.where(own_half, g_upb[None], 0.0).reshape(-1)
    small_grads = jnp.concatenate(
        [
            norm_rows,
            fold(qb_full, dp_size, rows, sizes.qb_cols),
            fold(ub_full, dp_size, rows, sizes.ub_cols),
        ],
        axis=2,
    )
    small_grads = jnp.pad(
        small_grads,
        (
            (0, 0),
            (0, 0),
            (sizes.small - sizes.tile, sizes.tile_end - sizes.small - sizes.n_small),
        ),
    ).reshape(dp_size // 2, 2, rows, -1)

    def turned(values):
        return values.T.reshape(dp_size // 2, 2, rows, count)

    operands = (
        turned(n2),
        turned(cot),
        turned(n1),
        du,
        act,
        jnp.pad(d_qkv, ((0, 0), (0, sizes.out - sizes.small))),
        jnp.pad(attended_flat, ((0, 0), (0, sizes.cols - sizes.out - out_q))),
        small_grads,
    )
    parts = jnp.concatenate([mixed.astype(BF16), back.astype(BF16)], axis=1)
    parts = parts.reshape(2, 2, own, 2 * width)
    reduced, sums, small_sum = scatter(sizes, n_outer, operands, parts)

    own_x = tokens.astype(F32)
    own_unit, own_inv = unit_rows(own_x)
    hidden = (own_x + sums[:, :width] + vecs[4] + vecs[5]).astype(BF16)
    total = sums[:, width:]
    mean_term = jnp.mean(total, axis=-1, keepdims=True)
    proj_term = jnp.mean(total * own_unit, axis=-1, keepdims=True)
    input_grad = up_rows + own_inv * (total - mean_term - own_unit * proj_term)

    def columns(start, size):
        return jnp.swapaxes(reduced[:, :, start : start + size], 0, 1).reshape(rows, 2 * size)

    def columns_t(start, size):
        return jnp.swapaxes(reduced[:, :, start : start + size], 1, 2).reshape(2 * size, rows)

    off = sizes.small - sizes.tile
    fin = small_sum[1, :, off : off + 6].T
    qb_out = small_sum[0, :, off + 6 : off + 6 + sizes.qb_cols].reshape(-1)[: sizes.qkvb]
    ub_at = off + 6 + sizes.qb_cols
    ub_out = small_sum[0, :, ub_at : ub_at + sizes.ub_cols].reshape(-1)[: sizes.upb]
    return (
        hidden[None],
        input_grad,
        columns(sizes.qkv, qkv_q)[None],
        qb_out[None],
        columns_t(sizes.out, out_q)[None],
        fin[4][None],
        columns(0, up_q)[None],
        ub_out[None],
        columns_t(sizes.down, up_q)[None],
        fin[4][None],
        fin[0][None],
        fin[1][None],
        fin[2][None],
        fin[3][None],
    )


def solution(mesh):
    in_specs = (
        P(("dp", "tensor"), None),
        P("dp"),
        P("dp"),
        P(("dp", "tensor"), None),
        P(None, "dp", "tensor"),
        P(None, ("tensor", "dp")),
        P(None, "tensor", "dp"),
        P(None, "dp"),
        P(None, "dp", "tensor"),
        P(None, ("tensor", "dp")),
        P(None, "tensor", "dp"),
        P(None, "dp"),
        P(None, "dp"),
        P(None, "dp"),
        P(None, "dp"),
        P(None, "dp"),
    )
    out_specs = (
        P(None, ("dp", "tensor"), None),
        P(("dp", "tensor"), None),
        P(None, "dp", "tensor"),
        P(None, ("tensor", "dp")),
        P(None, "tensor", "dp"),
        P(None, "dp"),
        P(None, "dp", "tensor"),
        P(None, ("tensor", "dp")),
        P(None, "tensor", "dp"),
        P(None, "dp"),
        P(None, "dp"),
        P(None, "dp"),
        P(None, "dp"),
        P(None, "dp"),
    )
    return jax.shard_map(
        on_device, mesh=mesh, in_specs=in_specs, out_specs=out_specs, check_vma=False
    )
```

time: 532 us -> 175 us (0.33)
  the two profiles are of different devices: /device:TPU:13 before, /device:TPU:1 now
where the time goes in v1:
time: 175 us; the launch traced here: 174 us
  Pallas kernels  112 us (64%)
  local copies, waits for them, and re-layouts  30.3 us (17%)
  matrix products  21.2 us (12%)
  other arithmetic  9.17 us (5%)
    pallas_call x1, Pallas kernels, scatter(): pl.pallas_call(functools.partial(scatter_kernel, sizes, n_outer), out_sha...  58.4 us
    pallas_call x1, Pallas kernels, gather(): pl.pallas_call(functools.partial(gather_kernel, n_outer), out_shape=(jax....  53.8 us
    dot_general x8, matrix products, dot(): lax.dot_general(a, b, (((ca,), (cb,)), ((), ())), preferred_element_type=...  18.8 us
    unnamed x89, local copies, waits for them, and re-layouts  6.42 us
    transpose x4, local copies, waits for them, and re-layouts, turned(): return values.T.reshape(dp_size // 2, 2, rows, count)  3.59 us

profile of v1, /device:TPU:1, one launch (start us, length us, event | category | flops | bytes accessed | tf_op | source)
XLA Modules:
  0.0 174.4 jit_solution(4427425166900174446)
XLA Ops:
  0.8 1.1 reshape_squeeze.13
  1.9 0.9 reshape_squeeze.14
  2.9 1.1 reshape_squeeze.15
  5.4 0.7 reduce.22
  6.5 0.9 concatenate.52.p_ref
  7.6 0.8 fusion.37.a_ref
  8.4 53.8 %gather.1 = (bf16[8,2,48,2432]{3,2,1,0:T(8,128)(2,1)}, bf16[2,2,128,1664]{3,2,1,0:T(8,128)(2,1)}) custom-call(bf16[2,48,2432]{2,1,0:T(8,128)(2,1)} %concatenate.52.p_ref, bf16[128,1664]{1,0:T(8,128)(2,1)} %fusion.37.a_ref), custom_call_target="tpu_custom_call" | custom-call | tf_op jit(solution)/shard_map/gather/pallas_call | solution.py:334
  62.2 1.2 slice.220
  64.9 3.4 %multiply_convert_fusion.1 = (bf16[512,768]{1,0:T(8,128)(2,1)}, f32[512,768]{1,0:T(8,128)S(1)}) fusion(f32[768]{0:T(1024)S(1)} %dynamic_slice.10, bf16[768,2432]{1,0:T(8,128)(2,1)} %bitcast.147, f32[768]{0:T(1024)S(1)} %get-tuple-element.104, f32[768]{0:T(1024)S(1)} %get-tuple-element.105, f32[512]{0:T(512)S(1)} %add_rsqrt_fusion, ...), kind=kOutput, calls=%fused_computation.30 | convolution fusion | flops 608698368 | bytes 4341760 | tf_op jit(solution)/shard_map/dot_general | solution.py:433
  68.3 1.1 convert_reduce_fusion.1
  69.4 2.0 %fusion.21 = f32[512,768]{1,0:T(8,128)} fusion(bf16[512,768]{1,0:T(8,128)(2,1)S(1)} %get-tuple-element.147.du_ref, bf16[768,2432]{1,0:T(8,128)(2,1)S(1)} %bitcast.154), kind=kOutput, calls=%fused_computation.41 | convolution fusion | flops 603979776 | bytes 3538944 | tf_op jit(solution)/shard_map/dot_general | solution.py:433
  71.8 3.1 %convolution_add_fusion.1 = f32[512,576]{0,1:T(8,128)} fusion(bf16[768,2432]{1,0:T(8,128)(2,1)} %bitcast.148, f32[576]{0:T(1024)S(1)} %dynamic_slice.11, f32[768]{0:T(1024)S(1)} %get-tuple-element.102, f32[768]{0:T(1024)S(1)} %get-tuple-element.103, f32[512]{0:T(512)S(1)} %add_rsqrt_fusion, f32[512]{0:T(512)S(1)} %broadcast_multiply_fusion, ...), kind=kOutput, calls=%fused_computation.33 | convolution fusion | flops 455639040 | bytes 2965504 | tf_op jit(solution)/shard_map/dot_general | solution.py:433
  74.9 2.0 %reshape.205 = f32[2,256,3,3,64]{1,0,4,3,2:T(2,128)S(1)} reshape(f32[512,576]{0,1:T(8,128)} %convolution_add_fusion.1) | data formatting | bytes 2359296 | tf_op jit(solution)/shard_map/reshape | solution.py:542
  77.2 1.0 convert_reduce_fusion.5
  79.5 1.7 convolution_convert_fusion
  86.2 3.9 %fusion.11 = (f32[768]{0:T(1024)S(1)}, f32[768]{0:T(1024)S(1)}, f32[768]{0:T(1024)S(1)}, f32[768]{0:T(1024)S(1)}, bf16[512,768]{1,0:T(8,128)(2,1)}, /*index=5*/bf16[768,512]{0,1:T(8,128)(2,1)S(1)}, bf16[768,512]{0,1:T(8,128)(2,1)}) fusion(f32[512,768]{1,0:T(8,128)S(1)} %copy-done.33, f32[512]{0:T(512)S(1)} %copy-done.22, ...), kind=kOutput, calls=%fused_computation.14 | convolution fusion | flops 460452864 | bytes 6320128 | tf_op jit(solution)/shard_map/dot_general | solution.py:433
  90.2 1.2 copy.200
  91.4 1.2 copy.201
  92.6 1.2 copy.202
  94.1 0.9 pad.26.dqkv_ref
  95.4 0.7 pad.27.att_ref
  97.7 0.9 pad.29.clone
  98.6 1.4 fusion.45
  100.0 2.2 %add_convert_fusion.1 = bf16[512,768]{1,0:T(8,128)(2,1)S(1)} fusion(f32[512,768]{1,0:T(8,128)S(1)} %fusion.45, bf16[512,768]{1,0:T(8,128)(2,1)S(1)} %copy-done.8, bf16[768,2432]{1,0:T(8,128)(2,1)} %bitcast.152), kind=kOutput, calls=%fused_computation.24 | convolution fusion | flops 604766208 | bytes 4325376 | tf_op jit(solution)/shard_map/dot_general | solution.py:433
  102.2 1.3 pad_maximum_fusion
  103.5 58.4 %scatter.1 = (f32[2,48,2432]{2,1,0:T(8,128)}, f32[128,1536]{1,0:T(8,128)}, f32[2,48,128]{2,1,0:T(8,128)}) custom-call(bf16[8,2,48,512]{3,2,1,0:T(8,128)(2,1)} %bitcast.129, bf16[8,2,48,512]{3,2,1,0:T(8,128)(2,1)} %bitcast.130, bf16[8,2,48,512]{3,2,1,0:T(8,128)(2,1)} %bitcast.131, bf16[512,768]{1,0:T(8,128)(2,1)} %copy-done.9, ...), custom_call_target="tpu_custom_call" | custom-call | tf_op jit(solution)/shard_map/scatter/pallas_call | solution.py:365
  162.2 1.2 slice_reduce_fusion
  163.4 2.1 %convert_add_fusion.1 = (f32[128,768]{1,0:T(8,128)}, bf16[1,128,768]{2,1,0:T(8,128)(2,1)}) fusion(bf16[128,768]{1,0:T(8,128)(2,1)S(1)} %copy-done.4, bf16[128,768]{1,0:T(8,128)(2,1)S(1)} %copy-done, f32[128,1536]{1,0:T(8,128)} %get-tuple-element.21, f32[128]{0:T(128)S(1)} %broadcast_multiply_fusion.1, f32[128]{0:T(128)S(1)} %broadcast_multiply_fusion.2, ...), kind=kLoop, calls=%fused_computation.60 | loop fusion | flops 1277952 | bytes 1777664 | tf_op jit(solution)/shard_map/add | solution.py:636
  165.7 0.9 broadcast_in_dim_reshape.13
  167.4 0.8 broadcast_in_dim_reshape.14
  168.7 1.0 broadcast_in_dim_reshape.15
  170.6 1.0 broadcast_in_dim_reshape.16
  (196 shorter events, 17.8 us)
Async XLA Ops:
  0.6 7.0 %copy-start.3 = (bf16[128,768]{1,0:T(8,128)(2,1)S(1)}, bf16[128,768]{1,0:T(8,128)(2,1)}, u32[]{:S(2)}) copy-start(bf16[128,768]{1,0:T(8,128)(2,1)} %param.18) | copy-start | bytes 589828
  0.7 6.9 %copy-start = (bf16[128,768]{1,0:T(8,128)(2,1)S(1)}, bf16[128,768]{1,0:T(8,128)(2,1)}, u32[]{:S(2)}) copy-start(bf16[128,768]{1,0:T(8,128)(2,1)} %param.16) | copy-start | bytes 589828
  0.7 3.3 %copy-start.23 = (bf16[1,48]{1,0:T(2,128)(2,1)S(1)}, bf16[1,48]{1,0:T(2,128)(2,1)}, u32[]{:S(2)}) copy-start(bf16[1,48]{1,0:T(2,128)(2,1)} %param.27) | copy-start | bytes 292
  0.7 3.4 %copy-start.24 = (bf16[1,48]{1,0:T(2,128)(2,1)S(1)}, bf16[1,48]{1,0:T(2,128)(2,1)}, u32[]{:S(2)}) copy-start(bf16[1,48]{1,0:T(2,128)(2,1)} %param.28) | copy-start | bytes 292
  0.7 3.5 %copy-start.25 = (bf16[1,48]{1,0:T(2,128)(2,1)S(1)}, bf16[1,48]{1,0:T(2,128)(2,1)}, u32[]{:S(2)}) copy-start(bf16[1,48]{1,0:T(2,128)(2,1)} %param.29) | copy-start | bytes 292
  0.7 3.6 %copy-start.26 = (bf16[1,48]{1,0:T(2,128)(2,1)S(1)}, bf16[1,48]{1,0:T(2,128)(2,1)}, u32[]{:S(2)}) copy-start(bf16[1,48]{1,0:T(2,128)(2,1)} %param.30) | copy-start | bytes 292
  0.7 3.7 %copy-start.27 = (bf16[1,48]{1,0:T(2,128)(2,1)S(1)}, bf16[1,48]{1,0:T(2,128)(2,1)}, u32[]{:S(2)}) copy-start(bf16[1,48]{1,0:T(2,128)(2,1)} %param.22) | copy-start | bytes 292
  0.7 3.8 %copy-start.28 = (bf16[1,48]{1,0:T(2,128)(2,1)S(1)}, bf16[1,48]{1,0:T(2,128)(2,1)}, u32[]{:S(2)}) copy-start(bf16[1,48]{1,0:T(2,128)(2,1)} %param.26) | copy-start | bytes 292
  0.7 3.9 %copy-start.31 = (bf16[1,72]{1,0:T(2,128)(2,1)S(1)}, bf16[1,72]{1,0:T(2,128)(2,1)}, u32[]{:S(2)}) copy-start(bf16[1,72]{1,0:T(2,128)(2,1)} %param.20) | copy-start | bytes 436
  0.7 4.6 %copy-start.32 = (bf16[1,96]{1,0:T(2,128)(2,1)S(1)}, bf16[1,96]{1,0:T(2,128)(2,1)}, u32[]{:S(2)}) copy-start(bf16[1,96]{1,0:T(2,128)(2,1)} %param.24) | copy-start | bytes 580
  0.8 5.6 %copy-start.16 = (bf16[1,384,48]{1,2,0:T(8,128)(2,1)S(1)}, bf16[1,384,48]{1,2,0:T(8,128)(2,1)}, u32[]{:S(2)}) copy-start(bf16[1,384,48]{1,2,0:T(8,128)(2,1)} %param.21) | copy-start | bytes 110596
  0.8 6.6 %copy-start.30 = (s32[256]{0:T(256)S(1)}, s32[256]{0:T(256)}, u32[]{:S(2)}) copy-start(s32[256]{0:T(256)} %param.17) | copy-start | bytes 3076
  62.2 2.1 %copy-start.1 = (bf16[2,2,128,1664]{3,2,1,0:T(8,128)(2,1)S(1)}, bf16[2,2,128,1664]{3,2,1,0:T(8,128)(2,1)}, u32[]{:S(2)}) copy-start(bf16[2,2,128,1664]{3,2,1,0:T(8,128)(2,1)} %get-tuple-element.19) | copy-start | bytes 5111812
  64.3 4.0 %copy-start.17 = (f32[768]{0:T(1024)}, f32[768]{0:T(1024)S(1)}, u32[]{:S(2)}) copy-start(f32[768]{0:T(1024)S(1)} %get-tuple-element.104) | copy-start | bytes 9220
  64.3 4.0 %copy-start.19 = (f32[768]{0:T(1024)}, f32[768]{0:T(1024)S(1)}, u32[]{:S(2)}) copy-start(f32[768]{0:T(1024)S(1)} %get-tuple-element.105) | copy-start | bytes 9220
  64.9 6.9 %copy-start.21 = (f32[512]{0:T(512)}, f32[512]{0:T(512)S(1)}, u32[]{:S(2)}) copy-start(f32[512]{0:T(512)S(1)} %add_rsqrt_fusion) | copy-start | bytes 6148
  64.9 3.4 %copy-start.15 = (bf16[8,2,48,2432]{3,2,1,0:T(8,128)(2,1)S(1)}, bf16[8,2,48,2432]{3,2,1,0:T(8,128)(2,1)}, u32[]{:S(2)}) copy-start(bf16[8,2,48,2432]{3,2,1,0:T(8,128)(2,1)} %get-tuple-element.20) | copy-start | bytes 11206660
  69.4 2.1 %copy-start.9 = (bf16[512,768]{1,0:T(8,128)(2,1)}, bf16[512,768]{1,0:T(8,128)(2,1)S(1)}, u32[]{:S(2)}) copy-start(bf16[512,768]{1,0:T(8,128)(2,1)S(1)} %get-tuple-element.147.du_ref) | copy-start | bytes 2359300
  77.2 2.1 %copy-start.10 = (bf16[2,3,256,48]{2,3,1,0:T(8,128)(2,1)}, bf16[2,3,256,48]{2,3,1,0:T(8,128)(2,1)S(1)}, u32[]{:S(2)}) copy-start(bf16[2,3,256,48]{2,3,1,0:T(8,128)(2,1)S(1)} %slice.345) | copy-start | bytes 442372
  82.0 0.9 copy-start.13
  84.2 1.5 copy-start.2
  84.3 1.4 copy-start.18
  84.3 1.4 copy-start.20
  84.3 1.4 copy-start.22
  84.3 1.9 %copy-start.33 = (f32[512,768]{1,0:T(8,128)S(1)}, f32[512,768]{1,0:T(8,128)}, u32[]{:S(2)}) copy-start(f32[512,768]{1,0:T(8,128)} %fusion.21) | copy-start | bytes 4718596
  91.4 1.2 copy-start.6
  94.1 2.4 %copy-start.4 = (bf16[128,768]{1,0:T(8,128)(2,1)S(1)}, bf16[128,768]{1,0:T(8,128)(2,1)}, u32[]{:S(2)}) copy-start(bf16[128,768]{1,0:T(8,128)(2,1)} %param.18) | copy-start | bytes 589828
  97.7 2.3 %copy-start.8 = (bf16[512,768]{1,0:T(8,128)(2,1)S(1)}, bf16[512,768]{1,0:T(8,128)(2,1)}, u32[]{:S(2)}) copy-start(bf16[512,768]{1,0:T(8,128)(2,1)} %get-tuple-element.144.act_ref) | copy-start | bytes 2359300
  100.0 2.2 %copy-start.7 = (bf16[512,768]{1,0:T(8,128)(2,1)S(1)}, bf16[512,768]{1,0:T(8,128)(2,1)}, u32[]{:S(2)}) copy-start(bf16[512,768]{1,0:T(8,128)(2,1)} %get-tuple-element.108) | copy-start | bytes 2359300
  161.9 3.7 %copy-start.5 = (f32[2,48,2432]{2,1,0:T(8,128)S(1)}, f32[2,48,2432]{2,1,0:T(8,128)}, u32[]{:S(2)}) copy-start(f32[2,48,2432]{2,1,0:T(8,128)} %get-tuple-element.22) | copy-start | bytes 2801668
  163.4 3.2 %copy-start.14 = (f32[2,48,128]{2,1,0:T(8,128)S(1)}, f32[2,48,128]{2,1,0:T(8,128)}, u32[]{:S(2)}) copy-start(f32[2,48,128]{2,1,0:T(8,128)} %get-tuple-element.23) | copy-start | bytes 147460
  168.4 5.5 %copy-start.29 = (f32[1,48]{1,0:T(1,128)}, f32[1,48]{1,0:T(1,128)S(1)}, u32[]{:S(2)}) copy-start(f32[1,48]{1,0:T(1,128)S(1)} %copy.226) | copy-start | bytes 580
  (2 other events, 1.6 us)

commit v2 on v1

--- a/solution.py
+++ b/solution.py
@@ -182,8 +182,10 @@
     att_ref,
     small_ref,
     h_ref,
+    d_ref,
     r_ref,
     hs_ref,
+    ds_ref,
     x_ref,
     first_buf,
     b1,
@@ -229,7 +231,10 @@
         cut = lo - sizes.qkv
         put(sizes.qkv, lo, part[:, :, :cut])
         put(lo, hi, part[:, :, cut:] + small_ref[target])
-        put(sizes.out, sizes.cols, product(cott_ref, att_ref))
+        end = sizes.out + sizes.out_q
+        put(sizes.out, end, product(cott_ref, att_ref))
+        if end < sizes.cols:
+            put(end, sizes.cols, jnp.zeros((2, rows, sizes.cols - end), F32))
 
     def to_acc(start, stop, value):
         acc[:, :, start:stop] = value
@@ -238,9 +243,16 @@
     group = []
     spots = ((sibling, 1 - core, x), (across, core, 1 - x), (diagonal, 1 - core, 1 - x))
     for slot, (where, to_core, to_x) in enumerate(spots):
-        copy = rcopy(h_ref.at[to_core, to_x], hr.at[slot], grp_s.at[slot], grp_r.at[slot], where)
-        copy.start()
-        group.append(copy)
+        for kind, part in enumerate((h_ref, d_ref)):
+            copy = rcopy(
+                part.at[to_core, to_x],
+                hr.at[kind, slot],
+                grp_s.at[kind, slot],
+                grp_r.at[kind, slot],
+                where,
+            )
+            copy.start()
+            group.append(copy)
 
     def in_order(what):
         @pl.loop(0, last)
@@ -289,12 +301,13 @@
     in_order(send_second)
     for copy in group:
         copy.wait_recv()
-    hs_ref[...] = (
-        h_ref[core, x].astype(F32)
-        + hr[0].astype(F32)
-        + hr[1].astype(F32)
-        + hr[2].astype(F32)
-    )
+    for kind, (part, out) in enumerate(((h_ref, hs_ref), (d_ref, ds_ref))):
+        out[...] = (
+            part[core, x].astype(F32)
+            + hr[kind, 0].astype(F32)
+            + hr[kind, 1].astype(F32)
+            + hr[kind, 2].astype(F32)
+        )
     block(chip, to_acc)
     exchange(outer).wait_recv()
     acc[...] += b1[outer].astype(F32)
@@ -357,7 +370,7 @@
     )(packed, rows)
 
 
-def scatter(sizes, n_outer, operands, parts):
+def scatter(sizes, n_outer, operands, mixed, back):
     dma = pltpu.SemaphoreType.DMA
     full = pl.BlockSpec(memory_space=VMEM)
     block = (2, sizes.rows, sizes.cols)
@@ -366,22 +379,23 @@
         functools.partial(scatter_kernel, sizes, n_outer),
         out_shape=(
             jax.ShapeDtypeStruct(block, F32),
-            jax.ShapeDtypeStruct(parts.shape[2:], F32),
+            jax.ShapeDtypeStruct(mixed.shape[2:], F32),
+            jax.ShapeDtypeStruct(mixed.shape[2:], F32),
             jax.ShapeDtypeStruct((2, sizes.rows, width), F32),
         ),
-        in_specs=[full] * (len(operands) + 1),
-        out_specs=(full, full, full),
+        in_specs=[full] * (len(operands) + 2),
+        out_specs=(full, full, full, full),
         scratch_shapes=[
             VMEM((n_outer,) + block, BF16),
             VMEM((n_outer,) + block, BF16),
             VMEM((n_outer,) + block, BF16),
             VMEM((2, n_outer) + block, BF16),
             VMEM(block, F32),
-            VMEM((3,) + parts.shape[2:], BF16),
+            VMEM((2, 3) + mixed.shape[2:], BF16),
             VMEM((sizes.rows, width), F32),
             VMEM((sizes.rows, width), F32),
-            dma((3,)),
-            dma((3,)),
+            dma((2, 3)),
+            dma((2, 3)),
             dma((n_outer,)),
             dma((n_outer,)),
             dma((2, n_outer)),
@@ -395,7 +409,7 @@
             collective_id=1, has_side_effects=True, vmem_limit_bytes=60 * 2**20
         ),
         name="scatter",
-    )(*operands, parts)
+    )(*operands, mixed, back)
 
 
 def rotary_tables(pos_ids):
@@ -620,17 +634,20 @@
         du,
         act,
         jnp.pad(d_qkv, ((0, 0), (0, sizes.out - sizes.small))),
-        jnp.pad(attended_flat, ((0, 0), (0, sizes.cols - sizes.out - out_q))),
+        attended_flat,
         small_grads,
     )
-    parts = jnp.concatenate([mixed.astype(BF16), back.astype(BF16)], axis=1)
-    parts = parts.reshape(2, 2, own, 2 * width)
-    reduced, sums, small_sum = scatter(sizes, n_outer, operands, parts)
+    reduced, mixed_sum, total, small_sum = scatter(
+        sizes,
+        n_outer,
+        operands,
+        mixed.astype(BF16).reshape(2, 2, own, width),
+        back.astype(BF16).reshape(2, 2, own, width),
+    )
 
     own_x = tokens.astype(F32)
     own_unit, own_inv = unit_rows(own_x)
-    hidden = (own_x + sums[:, :width] + vecs[4] + vecs[5]).astype(BF16)
-    total = sums[:, width:]
+    hidden = (own_x + mixed_sum + vecs[4] + vecs[5]).astype(BF16)
     mean_term = jnp.mean(total, axis=-1, keepdims=True)
     proj_term = jnp.mean(total * own_unit, axis=-1, keepdims=True)
     input_grad = up_rows + own_inv * (total - mean_term - own_unit * proj_term)

time: 175 us -> 174 us (level)
    unnamed x89 -> x87, local copies, waits for them, and re-layouts: 6.42 us -> 6.41 us
where the time goes in v2:
time: 174 us
  Pallas kernels  112 us (64%)
  local copies, waits for them, and re-layouts  30.2 us (17%)
  matrix products  22 us (13%)
  other arithmetic  7.91 us (5%)
    pallas_call x1, Pallas kernels, scatter(): pl.pallas_call(functools.partial(scatter_kernel, sizes, n_outer), out_sha...  58.4 us
    pallas_call x1, Pallas kernels, gather(): pl.pallas_call(functools.partial(gather_kernel, n_outer), out_shape=(jax....  53.9 us
    dot_general x8, matrix products, dot(): lax.dot_general(a, b, (((ca,), (cb,)), ((), ())), preferred_element_type=...  19.7 us
    unnamed x87, local copies, waits for them, and re-layouts  6.41 us
    transpose x4, local copies, waits for them, and re-layouts, turned(): return values.T.reshape(dp_size // 2, 2, rows, count)  3.59 us

profile of v2, /device:TPU:1, one launch (start us, length us, event | category | flops | bytes accessed | tf_op | source)
XLA Modules:
  0.0 173.9 jit_solution(16650005428959587235)
XLA Ops:
  0.8 1.1 reshape_squeeze.13
  1.9 0.9 reshape_squeeze.14
  2.9 1.1 reshape_squeeze.15
  5.4 0.7 reduce.22
  6.5 0.9 concatenate.49.p_ref
  7.6 0.8 fusion.37.a_ref
  8.4 53.9 %gather.1 = (bf16[8,2,48,2432]{3,2,1,0:T(8,128)(2,1)}, bf16[2,2,128,1664]{3,2,1,0:T(8,128)(2,1)}) custom-call(bf16[2,48,2432]{2,1,0:T(8,128)(2,1)} %concatenate.49.p_ref, bf16[128,1664]{1,0:T(8,128)(2,1)} %fusion.37.a_ref), custom_call_target="tpu_custom_call" | custom-call | tf_op jit(solution)/shard_map/gather/pallas_call | solution.py:347
  62.3 1.2 slice.212
  64.9 3.3 %multiply_convert_fusion.1 = (bf16[512,768]{1,0:T(8,128)(2,1)}, f32[512,768]{1,0:T(8,128)S(1)}) fusion(f32[768]{0:T(1024)S(1)} %dynamic_slice.10, bf16[768,2432]{1,0:T(8,128)(2,1)} %bitcast.149, f32[768]{0:T(1024)S(1)} %get-tuple-element.106, f32[768]{0:T(1024)S(1)} %get-tuple-element.107, f32[512]{0:T(512)S(1)} %add_rsqrt_fusion, ...), kind=kOutput, calls=%fused_computation.29 | convolution fusion | flops 608698368 | bytes 4341760 | tf_op jit(solution)/shard_map/dot_general | solution.py:447
  68.3 1.1 convert_reduce_fusion.1
  69.4 2.0 %fusion.21 = f32[512,768]{1,0:T(8,128)} fusion(bf16[512,768]{1,0:T(8,128)(2,1)S(1)} %get-tuple-element.149.du_ref, bf16[768,2432]{1,0:T(8,128)(2,1)S(1)} %bitcast.156), kind=kOutput, calls=%fused_computation.40 | convolution fusion | flops 603979776 | bytes 3538944 | tf_op jit(solution)/shard_map/dot_general | solution.py:447
  71.7 3.2 %convolution_add_fusion.1 = f32[512,576]{0,1:T(8,128)} fusion(bf16[768,2432]{1,0:T(8,128)(2,1)} %bitcast.150, f32[576]{0:T(1024)S(1)} %dynamic_slice.11, f32[768]{0:T(1024)S(1)} %get-tuple-element.104, f32[768]{0:T(1024)S(1)} %get-tuple-element.105, f32[512]{0:T(512)S(1)} %add_rsqrt_fusion, f32[512]{0:T(512)S(1)} %broadcast_multiply_fusion, ...), kind=kOutput, calls=%fused_computation.32 | convolution fusion | flops 455639040 | bytes 2965504 | tf_op jit(solution)/shard_map/dot_general | solution.py:447
  74.9 2.0 %reshape.208 = f32[2,256,3,3,64]{1,0,4,3,2:T(2,128)S(1)} reshape(f32[512,576]{0,1:T(8,128)} %convolution_add_fusion.1) | data formatting | bytes 2359296 | tf_op jit(solution)/shard_map/reshape | solution.py:556
  77.2 1.0 convert_reduce_fusion.5
  79.5 1.7 convolution_convert_fusion
  86.2 4.0 %fusion.11 = (f32[768]{0:T(1024)S(1)}, f32[768]{0:T(1024)S(1)}, f32[768]{0:T(1024)S(1)}, f32[768]{0:T(1024)S(1)}, bf16[512,768]{1,0:T(8,128)(2,1)}, /*index=5*/bf16[768,512]{0,1:T(8,128)(2,1)S(1)}, bf16[768,512]{0,1:T(8,128)(2,1)}) fusion(f32[512,768]{1,0:T(8,128)S(1)} %copy-done.32, f32[512]{0:T(512)S(1)} %copy-done.21, ...), kind=kOutput, calls=%fused_computation.14 | convolution fusion | flops 460452864 | bytes 6320128 | tf_op jit(solution)/shard_map/dot_general | solution.py:447
  90.2 1.2 copy.200
  91.4 1.2 copy.201
  92.6 1.2 copy.202
  94.1 0.9 pad.22.dqkv_ref
  95.3 0.8 copy.221.att_ref
  97.7 0.9 pad.24.clone
  98.6 1.4 fusion.45
  100.0 3.0 %add_convert_fusion.1 = bf16[512,768]{1,0:T(8,128)(2,1)} fusion(f32[512,768]{1,0:T(8,128)S(1)} %fusion.45, bf16[512,768]{1,0:T(8,128)(2,1)S(1)} %copy-done.7, bf16[768,2432]{1,0:T(8,128)(2,1)} %bitcast.154), kind=kOutput, calls=%fused_computation.23 | convolution fusion | flops 604766208 | bytes 4325376 | tf_op jit(solution)/shard_map/dot_general | solution.py:447
  103.0 58.4 %scatter.1 = (f32[2,48,2432]{2,1,0:T(8,128)}, f32[128,768]{1,0:T(8,128)}, f32[128,768]{1,0:T(8,128)}, f32[2,48,128]{2,1,0:T(8,128)}) custom-call(bf16[8,2,48,512]{3,2,1,0:T(8,128)(2,1)} %bitcast.129, bf16[8,2,48,512]{3,2,1,0:T(8,128)(2,1)} %bitcast.130, bf16[8,2,48,512]{3,2,1,0:T(8,128)(2,1)} %bitcast.131, bf16[512,768]{1,0:T(8,128)(2,1)} %copy-done.8, ...), custom_call_target="tpu_custom_call" | custom-call | tf_op jit(solution)/shard_map/scatter/pallas_call | solution.py:378
  161.8 1.2 fusion.73
  163.0 2.1 %convert_add_fusion.1 = (f32[128,768]{1,0:T(8,128)}, bf16[1,128,768]{2,1,0:T(8,128)(2,1)}) fusion(bf16[128,768]{1,0:T(8,128)(2,1)S(1)} %copy-done.4, bf16[128,768]{1,0:T(8,128)(2,1)S(1)} %copy-done, f32[128,768]{1,0:T(8,128)} %get-tuple-element.23, f32[128]{0:T(128)S(1)} %broadcast_multiply_fusion.1, f32[128]{0:T(128)S(1)} %broadcast_multiply_fusion.2, ...), kind=kLoop, calls=%fused_computation.59 | loop fusion | flops 1277952 | bytes 1777664 | tf_op jit(solution)/shard_map/add | solution.py:653
  165.3 0.9 broadcast_in_dim_reshape.13
  166.9 0.8 broadcast_in_dim_reshape.14
  168.2 1.0 broadcast_in_dim_reshape.15
  169.3 0.6 broadcast_in_dim_reshape_squeeze.3
  170.1 1.0 broadcast_in_dim_reshape.16
  (192 shorter events, 17.1 us)
Async XLA Ops:
  0.6 6.9 %copy-start.3 = (bf16[128,768]{1,0:T(8,128)(2,1)S(1)}, bf16[128,768]{1,0:T(8,128)(2,1)}, u32[]{:S(2)}) copy-start(bf16[128,768]{1,0:T(8,128)(2,1)} %param.18) | copy-start | bytes 589828
  0.7 6.9 %copy-start = (bf16[128,768]{1,0:T(8,128)(2,1)S(1)}, bf16[128,768]{1,0:T(8,128)(2,1)}, u32[]{:S(2)}) copy-start(bf16[128,768]{1,0:T(8,128)(2,1)} %param.16) | copy-start | bytes 589828
  0.7 3.3 %copy-start.22 = (bf16[1,48]{1,0:T(2,128)(2,1)S(1)}, bf16[1,48]{1,0:T(2,128)(2,1)}, u32[]{:S(2)}) copy-start(bf16[1,48]{1,0:T(2,128)(2,1)} %param.27) | copy-start | bytes 292
  0.7 3.4 %copy-start.23 = (bf16[1,48]{1,0:T(2,128)(2,1)S(1)}, bf16[1,48]{1,0:T(2,128)(2,1)}, u32[]{:S(2)}) copy-start(bf16[1,48]{1,0:T(2,128)(2,1)} %param.28) | copy-start | bytes 292
  0.7 3.5 %copy-start.24 = (bf16[1,48]{1,0:T(2,128)(2,1)S(1)}, bf16[1,48]{1,0:T(2,128)(2,1)}, u32[]{:S(2)}) copy-start(bf16[1,48]{1,0:T(2,128)(2,1)} %param.29) | copy-start | bytes 292
  0.7 3.6 %copy-start.25 = (bf16[1,48]{1,0:T(2,128)(2,1)S(1)}, bf16[1,48]{1,0:T(2,128)(2,1)}, u32[]{:S(2)}) copy-start(bf16[1,48]{1,0:T(2,128)(2,1)} %param.30) | copy-start | bytes 292
  0.7 3.7 %copy-start.26 = (bf16[1,48]{1,0:T(2,128)(2,1)S(1)}, bf16[1,48]{1,0:T(2,128)(2,1)}, u32[]{:S(2)}) copy-start(bf16[1,48]{1,0:T(2,128)(2,1)} %param.22) | copy-start | bytes 292
  0.7 3.8 %copy-start.27 = (bf16[1,48]{1,0:T(2,128)(2,1)S(1)}, bf16[1,48]{1,0:T(2,128)(2,1)}, u32[]{:S(2)}) copy-start(bf16[1,48]{1,0:T(2,128)(2,1)} %param.26) | copy-start | bytes 292
  0.7 3.9 %copy-start.30 = (bf16[1,72]{1,0:T(2,128)(2,1)S(1)}, bf16[1,72]{1,0:T(2,128)(2,1)}, u32[]{:S(2)}) copy-start(bf16[1,72]{1,0:T(2,128)(2,1)} %param.20) | copy-start | bytes 436
  0.7 4.6 %copy-start.31 = (bf16[1,96]{1,0:T(2,128)(2,1)S(1)}, bf16[1,96]{1,0:T(2,128)(2,1)}, u32[]{:S(2)}) copy-start(bf16[1,96]{1,0:T(2,128)(2,1)} %param.24) | copy-start | bytes 580
  0.8 5.6 %copy-start.15 = (bf16[1,384,48]{1,2,0:T(8,128)(2,1)S(1)}, bf16[1,384,48]{1,2,0:T(8,128)(2,1)}, u32[]{:S(2)}) copy-start(bf16[1,384,48]{1,2,0:T(8,128)(2,1)} %param.21) | copy-start | bytes 110596
  0.8 6.6 %copy-start.29 = (s32[256]{0:T(256)S(1)}, s32[256]{0:T(256)}, u32[]{:S(2)}) copy-start(s32[256]{0:T(256)} %param.17) | copy-start | bytes 3076
  62.2 2.1 %copy-start.1 = (bf16[2,2,128,1664]{3,2,1,0:T(8,128)(2,1)S(1)}, bf16[2,2,128,1664]{3,2,1,0:T(8,128)(2,1)}, u32[]{:S(2)}) copy-start(bf16[2,2,128,1664]{3,2,1,0:T(8,128)(2,1)} %get-tuple-element.20) | copy-start | bytes 5111812
  64.3 3.9 %copy-start.16 = (f32[768]{0:T(1024)}, f32[768]{0:T(1024)S(1)}, u32[]{:S(2)}) copy-start(f32[768]{0:T(1024)S(1)} %get-tuple-element.106) | copy-start | bytes 9220
  64.3 3.9 %copy-start.18 = (f32[768]{0:T(1024)}, f32[768]{0:T(1024)S(1)}, u32[]{:S(2)}) copy-start(f32[768]{0:T(1024)S(1)} %get-tuple-element.107) | copy-start | bytes 9220
  64.9 6.8 %copy-start.20 = (f32[512]{0:T(512)}, f32[512]{0:T(512)S(1)}, u32[]{:S(2)}) copy-start(f32[512]{0:T(512)S(1)} %add_rsqrt_fusion) | copy-start | bytes 6148
  64.9 3.3 %copy-start.14 = (bf16[8,2,48,2432]{3,2,1,0:T(8,128)(2,1)S(1)}, bf16[8,2,48,2432]{3,2,1,0:T(8,128)(2,1)}, u32[]{:S(2)}) copy-start(bf16[8,2,48,2432]{3,2,1,0:T(8,128)(2,1)} %get-tuple-element.21) | copy-start | bytes 11206660
  69.4 2.0 %copy-start.8 = (bf16[512,768]{1,0:T(8,128)(2,1)}, bf16[512,768]{1,0:T(8,128)(2,1)S(1)}, u32[]{:S(2)}) copy-start(bf16[512,768]{1,0:T(8,128)(2,1)S(1)} %get-tuple-element.149.du_ref) | copy-start | bytes 2359300
  77.2 2.1 %copy-start.9 = (bf16[2,3,256,48]{2,3,1,0:T(8,128)(2,1)}, bf16[2,3,256,48]{2,3,1,0:T(8,128)(2,1)S(1)}, u32[]{:S(2)}) copy-start(bf16[2,3,256,48]{2,3,1,0:T(8,128)(2,1)S(1)} %slice.331) | copy-start | bytes 442372
  82.0 0.9 copy-start.12
  82.9 0.9 copy-start.10
  84.2 1.5 copy-start.2
  84.3 1.4 copy-start.17
  84.3 1.4 copy-start.19
  84.3 1.4 copy-start.21
  84.3 1.9 %copy-start.32 = (f32[512,768]{1,0:T(8,128)S(1)}, f32[512,768]{1,0:T(8,128)}, u32[]{:S(2)}) copy-start(f32[512,768]{1,0:T(8,128)} %fusion.21) | copy-start | bytes 4718596
  91.4 1.2 copy-start.6
  94.1 2.3 %copy-start.4 = (bf16[128,768]{1,0:T(8,128)(2,1)S(1)}, bf16[128,768]{1,0:T(8,128)(2,1)}, u32[]{:S(2)}) copy-start(bf16[128,768]{1,0:T(8,128)(2,1)} %param.18) | copy-start | bytes 589828
  97.7 2.3 %copy-start.7 = (bf16[512,768]{1,0:T(8,128)(2,1)S(1)}, bf16[512,768]{1,0:T(8,128)(2,1)}, u32[]{:S(2)}) copy-start(bf16[512,768]{1,0:T(8,128)(2,1)} %get-tuple-element.146.act_ref) | copy-start | bytes 2359300
  161.4 3.7 %copy-start.5 = (f32[2,48,2432]{2,1,0:T(8,128)S(1)}, f32[2,48,2432]{2,1,0:T(8,128)}, u32[]{:S(2)}) copy-start(f32[2,48,2432]{2,1,0:T(8,128)} %get-tuple-element.24) | copy-start | bytes 2801668
  163.0 3.2 %copy-start.13 = (f32[2,48,128]{2,1,0:T(8,128)S(1)}, f32[2,48,128]{2,1,0:T(8,128)}, u32[]{:S(2)}) copy-start(f32[2,48,128]{2,1,0:T(8,128)} %get-tuple-element.25) | copy-start | bytes 147460
  167.9 5.5 %copy-start.28 = (f32[1,48]{1,0:T(1,128)}, f32[1,48]{1,0:T(1,128)S(1)}, u32[]{:S(2)}) copy-start(f32[1,48]{1,0:T(1,128)S(1)} %copy.226) | copy-start | bytes 580
  (1 other events, 0.7 us)
